TPU v7x, 32 devices: a whole 2x2x4 slice. The times are simulated.
32 devices in a mesh: groups: 2 (over y), tm: 4 (over z), band: 2 (over x), tmpl: 2 (over core).
Axes of the slice: x: 2, y: 2, z: 4, core: 2. Of those that a mesh axis runs over, the one named last changes fastest.
Arguments:
- sft_bins: float32 [2, 128, 2048], P(None, ('groups', 'tm'), 'band'), parts along dimension 1, may hold values from -6 to 6
- delay_code: int32 [8, 128, 1024], P(('groups', 'tmpl'), None, ('tm', 'band')), parts along dimension 0, may hold values from 0 to 16007, as said below
- antenna: float32 [8, 2, 128, 1024], P(('groups', 'tmpl'), None, None, ('tm', 'band')), parts along dimension 0, may hold values from -10 to 10
Outputs:
- f_stat: float32 [8, 128, 8, 128], P(('groups', 'tmpl'), None, ('tm', 'band')), parts along dimension 0
There are 2 independent parts, one for each index of `groups`. A program takes and returns all parts, laid end to end along the dimension named above; each array names one. Nothing has to cross between parts.
Inputs may be any that keep to these rules, and one draw needn't show every extreme that they name: `delay_code`: the whole delay o of a template is the same for all samples n of each aligned run of 256 samples (n // 256 equal).
All inputs are finite; a program needn't handle non-finite values.
Results may differ from a plain program's by a relative error of at most 0.0003.
Values sent between devices are 32-bit elements; how exact they have to be, the bound alone decides.
No kernel may reach another device: no remote copies, remote signals or barrier semaphores. Data moves between devices by JAX's collectives and lax.ppermute only.
A program may use at most 64 MiB of HBM per device.

v0:
```python
import math

import jax
import jax.numpy as jnp
from jax import lax
from jax.sharding import PartitionSpec as P

NB = 2048
NQ = 128
NP = 16
SFT_DEV = 8
MAXD = 1000
NFRAC = 8
RUN = 256


stat_eps = 1e-06
floor_share = 0.5


def shifted(value, axis, by):
    length = lax.axis_size(axis)
    pairs = [(i, i + by) for i in range(length) if 0 <= i + by < length]
    return lax.ppermute(value, axis, pairs)


def lagrange(fraction):
    return (
        -fraction * (fraction - 1.0) * (fraction - 2.0) / 6.0,
        (fraction + 1.0) * (fraction - 1.0) * (fraction - 2.0) / 2.0,
        -(fraction + 1.0) * fraction * (fraction - 2.0) / 2.0,
        (fraction + 1.0) * fraction * (fraction - 1.0) / 6.0,
    )


def phase_pair(product, modulus, direction):
    angles = direction * 2.0 * math.pi / modulus * (product % modulus).astype(jnp.float32)
    return (jnp.cos(angles), jnp.sin(angles))


def dft_table(length, direction):
    rows_at = lax.broadcasted_iota(jnp.int32, (length, length), 0)
    cols_at = lax.broadcasted_iota(jnp.int32, (length, length), 1)
    return phase_pair(rows_at * cols_at, length, direction)


def complex_einsum(pattern, lhs_pair, rhs_pair):
    lhs_real, lhs_imag = lhs_pair
    rhs_real, rhs_imag = rhs_pair
    high = lax.Precision.HIGHEST
    out_real = jnp.einsum(pattern, lhs_real, rhs_real, precision=high) - jnp.einsum(
        pattern, lhs_imag, rhs_imag, precision=high
    )
    out_imag = jnp.einsum(pattern, lhs_real, rhs_imag, precision=high) + jnp.einsum(
        pattern, lhs_imag, rhs_real, precision=high
    )
    return (out_real, out_imag)


def rotate(values, phases):
    val_real, val_imag = values
    cos_part, sin_part = phases
    return (val_real * cos_part - val_imag * sin_part, val_real * sin_part + val_imag * cos_part)


def apply_weights(arrived):
    return arrived[:, 1][:, :, None] * arrived[:, 0][:, None]


def finish(arrived):
    owners = lax.axis_size("tm") * lax.axis_size("band")
    my_rank = lax.axis_index("tm") * lax.axis_size("band") + lax.axis_index("band")
    q_local = arrived.shape[3]
    lane_width = arrived.shape[5]
    sample_total = SFT_DEV * owners * NB
    section_one = complex_einsum(
        "abqix,ic->abqcx", (arrived[:, :, 0], arrived[:, :, 1]), dft_table(owners, -1.0)
    )
    c_pos = lax.broadcasted_iota(jnp.int32, (owners, lane_width), 0)
    x_pos = lax.broadcasted_iota(jnp.int32, (owners, lane_width), 1)
    section_one = rotate(section_one, phase_pair(c_pos * (x_pos // NP), SFT_DEV * owners, -1.0))
    short_table = dft_table(SFT_DEV, -1.0)
    ident_rows = jnp.eye(NP, dtype=jnp.float32)
    spread = (jnp.kron(short_table[0], ident_rows), jnp.kron(short_table[1], ident_rows))
    section_two = complex_einsum("abqcx,xy->abqcy", section_one, spread)
    q_grid = my_rank * q_local + lax.broadcasted_iota(jnp.int32, (q_local, owners, lane_width), 0)
    c_grid = lax.broadcasted_iota(jnp.int32, (q_local, owners, lane_width), 1)
    x_grid = lax.broadcasted_iota(jnp.int32, (q_local, owners, lane_width), 2)
    time_index = x_grid % NP + NP * q_grid
    freq_index = c_grid + owners * (x_grid // NP)
    section_two = rotate(section_two, phase_pair(time_index * freq_index, sample_total, -1.0))
    packed = jnp.stack(section_two, axis=2)
    turned = lax.all_to_all(packed, ("tm", "band"), split_axis=4, concat_axis=3, tiled=True)
    turned = turned.reshape(turned.shape[0], 2, 2, NQ, lane_width)
    section_three = complex_einsum(
        "abqx,qv->abvx", (turned[:, :, 0], turned[:, :, 1]), dft_table(NQ, -1.0)
    )
    v_pos = lax.broadcasted_iota(jnp.int32, (NQ, lane_width), 0)
    p_pos = lax.broadcasted_iota(jnp.int32, (NQ, lane_width), 1) % NP
    section_three = rotate(section_three, phase_pair(v_pos * p_pos, NB, -1.0))
    fine_table = dft_table(NP, -1.0)
    ident_blocks = jnp.eye(SFT_DEV, dtype=jnp.float32)
    block_table = (jnp.kron(ident_blocks, fine_table[0]), jnp.kron(ident_blocks, fine_table[1]))
    result = complex_einsum("abvx,xy->abvy", section_three, block_table)
    return jnp.stack(result, axis=2)


def per_device(sft_bins, delay_code, antenna):
    owners = lax.axis_size("tm") * lax.axis_size("band")
    sample_total = SFT_DEV * owners * NB
    spectra = lax.all_to_all(sft_bins, "band", split_axis=1, concat_axis=2, tiled=True)
    bin_grid = spectra.reshape(2, SFT_DEV, NP, NQ)
    section_one = complex_einsum("pk,skl->spl", dft_table(NP, 1.0), (bin_grid[0], bin_grid[1]))
    p_rows = lax.broadcasted_iota(jnp.int32, (NP, NQ), 0)
    l_cols = lax.broadcasted_iota(jnp.int32, (NP, NQ), 1)
    section_one = rotate(section_one, phase_pair(p_rows * l_cols, NB, 1.0))
    series_pair = complex_einsum("spl,lq->spq", section_one, dft_table(NQ, 1.0))
    norm_scale = 1.0 / math.sqrt(NB)
    stacked = jnp.stack([series_pair[0] * norm_scale, series_pair[1] * norm_scale])
    rim_cols = (MAXD + 1 + NP) // NP
    head_rim = stacked[:, 0, :, :rim_cols]
    tail_rim = stacked[:, SFT_DEV - 1, :, NQ - rim_cols :]
    after_rim = shifted(head_rim, ("tm", "band"), -1)
    before = shifted(tail_rim, ("tm", "band"), 1)
    rim_size = NP * rim_cols
    span_len = SFT_DEV * NB
    timed = stacked.transpose(0, 1, 3, 2).reshape(2, span_len)
    before_timed = before.transpose(0, 2, 1).reshape(2, rim_size)
    after_timed = after_rim.transpose(0, 2, 1).reshape(2, rim_size)
    buffer = jnp.concatenate([before_timed, timed, after_timed], axis=1)
    lane_width = SFT_DEV * NP
    tmpl_local = delay_code.shape[0]
    run_count = span_len // RUN
    code_time = (
        delay_code.reshape(tmpl_local, NQ, SFT_DEV, NP)
        .transpose(0, 2, 1, 3)
        .reshape(tmpl_local, run_count, RUN)
    )
    offsets = code_time[:, :, 0] // NFRAC - MAXD
    run_starts = (jnp.arange(run_count, dtype=jnp.int32) * RUN)[None, :] + offsets + (rim_size - 1)

    def take_segment(start):
        return lax.dynamic_slice_in_dim(buffer, start, RUN + 3, 1)

    segments = jax.vmap(jax.vmap(take_segment))(run_starts)
    fraction = (code_time % NFRAC).astype(jnp.float32) / NFRAC
    coeffs = lagrange(fraction)
    res_time = coeffs[0][:, :, None, :] * segments[:, :, :, 0:RUN]
    for tap_index in range(1, 4):
        res_time = (
            res_time
            + coeffs[tap_index][:, :, None, :] * segments[:, :, :, tap_index : tap_index + RUN]
        )
    resampled = res_time.transpose(0, 2, 1, 3).reshape(tmpl_local, 2, SFT_DEV, NQ, NP)
    resampled = resampled.transpose(0, 1, 3, 2, 4).reshape(tmpl_local, 2, NQ, lane_width)
    weight_a = antenna[:, 0]
    weight_b = antenna[:, 1]
    local_sums = jnp.stack(
        [
            jnp.sum(weight_a * weight_a, axis=(1, 2)),
            jnp.sum(weight_b * weight_b, axis=(1, 2)),
            jnp.sum(weight_a * weight_b, axis=(1, 2)),
        ],
        axis=1,
    )
    totals = lax.psum(local_sums, ("tm", "band"))
    payload = jnp.stack([resampled, antenna], axis=1)
    spectra_out = finish(
        apply_weights(
            lax.all_to_all(
                payload[:, :, :, :, None, :],
                ("tm", "band"),
                split_axis=3,
                concat_axis=4,
                tiled=True,
            )
        )
    )
    out_scale = 1.0 / math.sqrt(sample_total)
    a_real = spectra_out[:, 0, 0] * out_scale
    a_imag = spectra_out[:, 0, 1] * out_scale
    b_real = spectra_out[:, 1, 0] * out_scale
    b_imag = spectra_out[:, 1, 1] * out_scale
    power_a = (totals[:, 0] / sample_total + stat_eps)[:, None, None]
    power_b = (totals[:, 1] / sample_total + stat_eps)[:, None, None]
    cross_ab = (totals[:, 2] / sample_total)[:, None, None]
    det_floor = jnp.maximum(
        power_a * power_b - cross_ab * cross_ab, floor_share * power_a * power_b
    )
    f_stat = (
        power_b * (a_real * a_real + a_imag * a_imag)
        + power_a * (b_real * b_real + b_imag * b_imag)
        - 2.0 * cross_ab * (a_real * b_real + a_imag * b_imag)
    ) / det_floor
    return f_stat[:, :, None, :]


def solution(mesh):
    in_specs = (
        P(None, ("groups", "tm"), "band"),
        P(("groups", "tmpl"), None, ("tm", "band")),
        P(("groups", "tmpl"), None, None, ("tm", "band")),
    )
    out_specs = P(("groups", "tmpl"), None, ("tm", "band"), None)
    return jax.shard_map(
        per_device, mesh=mesh, in_specs=in_specs, out_specs=out_specs, check_vma=False
    )
```

profile of v0, /device:TPU:0, one launch (start us, length us, event | category | flops | bytes accessed | tf_op | source)
XLA Modules:
  0.0 251.6 jit_solution(13160571256986657289)
XLA Ops:
  0.0 1.7 copy.101
  1.7 4.2 %all-to-all-start = ((f32[2,16,1024]{2,0,1:T(2,128)}), f32[2,16,1024]{2,0,1:T(2,128)S(1)}, u32[]{:S(2)}, u32[]{:S(2)}) async-start(f32[2,16,1024]{2,0,1:T(2,128)} %copy.101), calls=%async_computation | async-start | bytes 262144 | tf_op jit(solution)/shard_map/all_to_all | solution.py:111
  6.1 1.8 copy.116
  7.9 1.1 multiply_reduce_fusion.2
  9.0 1.0 copy.99
  14.8 4.0 %collective-permute-start = (f32[2,16,63]{2,1,0:T(8,128)S(1)}, f32[2,16,63]{2,1,0:T(8,128)S(1)}, u32[]{:S(2)}, u32[]{:S(2)}) collective-permute-start(f32[2,16,63]{2,1,0:T(8,128)S(1)} %get-tuple-element.51), channel_id=1, source_target_pairs={{0,2},{2,4},{4,6},{6,8},{8,10},{10,12},{12,14},{1,3},{3,5},{5,7},{... | collective-permute-start | bytes 24200 | tf_op jit(solution)/shard_map/ppermute | solution.py:24
  18.8 1.3 collective-permute-start.1
  21.2 3.2 %collective-permute-done.1 = f32[2,16,63]{2,1,0:T(8,128)S(1)} collective-permute-done((f32[2,16,63]{2,1,0:T(8,128)S(1)}, f32[2,16,63]{2,1,0:T(8,128)S(1)}, u32[]{:S(2)}, u32[]{:S(2)}) %collective-permute-start.1) | collective-permute-done | bytes 8096 | tf_op jit(solution)/shard_map/ppermute | solution.py:24
  25.0 168.8 %while.1 = (s32[]{:T(128)}, f32[2,18400]{1,0:T(2,128)S(1)}, s32[128,2]{1,0:T(8,128)S(1)}, f32[128,2,259]{2,1,0:T(2,128)S(1)}, s32[]{:T(128)}) while((s32[]{:T(128)}, f32[2,18400]{1,0:T(2,128)S(1)}, s32[128,2]{1,0:T(8,128)S(1)}, f32[128,2,259]{2,1,0:T(2,128)S(1)}, s32[]{:T(128)}) %tuple.47), condition=%wide.while_cond, body=%wide.while_body.sunk | while | flops 2 | bytes 6241 | solution.py:143
  25.6 0.7 bitcast_dynamic-update-slice_fusion.2
  26.9 0.7 bitcast_dynamic-update-slice_fusion.2
  29.5 0.7 bitcast_dynamic-update-slice_fusion.2
  33.5 0.7 bitcast_dynamic-update-slice_fusion.2
  37.4 0.7 bitcast_dynamic-update-slice_fusion.2
  40.1 0.7 bitcast_dynamic-update-slice_fusion.2
  44.0 0.7 bitcast_dynamic-update-slice_fusion.2
  48.0 0.7 bitcast_dynamic-update-slice_fusion.2
  50.6 0.7 bitcast_dynamic-update-slice_fusion.2
  52.0 0.7 bitcast_dynamic-update-slice_fusion.2
  54.6 0.7 bitcast_dynamic-update-slice_fusion.2
  58.5 0.7 bitcast_dynamic-update-slice_fusion.2
  62.5 0.7 bitcast_dynamic-update-slice_fusion.2
  65.1 0.7 bitcast_dynamic-update-slice_fusion.2
  69.1 0.7 bitcast_dynamic-update-slice_fusion.2
  73.1 0.7 bitcast_dynamic-update-slice_fusion.2
  75.7 0.7 bitcast_dynamic-update-slice_fusion.2
  77.0 0.7 bitcast_dynamic-update-slice_fusion.2
  79.7 0.7 bitcast_dynamic-update-slice_fusion.2
  83.6 0.7 bitcast_dynamic-update-slice_fusion.2
  87.6 0.7 bitcast_dynamic-update-slice_fusion.2
  90.2 0.7 bitcast_dynamic-update-slice_fusion.2
  94.2 0.7 bitcast_dynamic-update-slice_fusion.2
  98.1 0.7 bitcast_dynamic-update-slice_fusion.2
  100.8 0.7 bitcast_dynamic-update-slice_fusion.2
  102.1 0.7 bitcast_dynamic-update-slice_fusion.2
  104.7 0.7 bitcast_dynamic-update-slice_fusion.2
  108.7 0.7 bitcast_dynamic-update-slice_fusion.2
  112.6 0.7 bitcast_dynamic-update-slice_fusion.2
  115.3 0.7 bitcast_dynamic-update-slice_fusion.2
  193.8 0.9 fusion.214
  196.0 1.0 maximum_bitcast_fusion
  197.0 1.0 copy.117
  198.0 5.8 %all-to-all-start.1 = ((f32[2,2,2,128,1,128]{5,2,0,1,4,3:T(2,128)}), f32[2,2,2,128,1,128]{5,2,0,1,4,3:T(2,128)S(1)}, u32[]{:S(2)}, u32[]{:S(2)}) async-start(f32[2,2,2,128,1,128]{5,2,0,1,4,3:T(2,128)} %copy.117), calls=%async_computation.1 | async-start | bytes 1048576 | tf_op jit(solution)/shard_map/all_to_all | solution.py:170
  203.8 22.1 %psum.7 = f32[2,3]{0,1:T(4,128)S(1)} all-reduce(f32[2,3]{0,1:T(4,128)S(1)} %pad_maximum_fusion.2), channel_id=1, replica_groups=mesh['groups'=2,'tm'=4,'band'=2,'tmpl'=2] {'tm','band'}, use_global_device_ids=true, to_apply=%region_3.4 | all-reduce | flops 6 | bytes 48 | tf_op jit(solution)/shard_map/psum | solution.py:166
  230.8 0.9 copy.123
  231.7 3.7 %all-to-all-start.2 = ((f32[2,2,2,16,8,128]{5,3,1,0,2,4:T(8,128)}), f32[2,2,2,16,8,128]{5,3,1,0,2,4:T(8,128)S(1)}, u32[]{:S(2)}, u32[]{:S(2)}) async-start(f32[2,2,2,16,8,128]{5,3,1,0,2,4:T(8,128)} %copy.123), calls=%async_computation.2 | async-start | bytes 1048576 | tf_op jit(solution)/shard_map/all_to_all | solution.py:93
  236.1 10.6 %all-to-all-done.2 = f32[2,2,2,16,8,128]{5,3,1,0,2,4:T(8,128)S(1)} async-done(((f32[2,2,2,16,8,128]{5,3,1,0,2,4:T(8,128)}), f32[2,2,2,16,8,128]{5,3,1,0,2,4:T(8,128)S(1)}, u32[]{:S(2)}, u32[]{:S(2)}) %all-to-all-start.2) | async-done | bytes 524320 | tf_op jit(solution)/shard_map/all_to_all | solution.py:93
  250.9 0.8 fusion.36
  (437 shorter events, 164.1 us)
Async XLA Ops:
  1.7 9.7 %all-to-all-start = ((f32[2,16,1024]{2,0,1:T(2,128)}), f32[2,16,1024]{2,0,1:T(2,128)S(1)}, u32[]{:S(2)}, u32[]{:S(2)}) async-start(f32[2,16,1024]{2,0,1:T(2,128)} %copy.101), calls=%async_computation | async-start | bytes 262144 | tf_op jit(solution)/shard_map/all_to_all | solution.py:111
  14.8 6.2 %collective-permute-start = (f32[2,16,63]{2,1,0:T(8,128)S(1)}, f32[2,16,63]{2,1,0:T(8,128)S(1)}, u32[]{:S(2)}, u32[]{:S(2)}) collective-permute-start(f32[2,16,63]{2,1,0:T(8,128)S(1)} %get-tuple-element.51), channel_id=1, source_target_pairs={{0,2},{2,4},{4,6},{6,8},{8,10},{10,12},{12,14},{1,3},{3,5},{5,7},{... | collective-permute-start | bytes 24200 | tf_op jit(solution)/shard_map/ppermute | solution.py:24
  18.8 5.6 %collective-permute-start.1 = (f32[2,16,63]{2,1,0:T(8,128)S(1)}, f32[2,16,63]{2,1,0:T(8,128)S(1)}, u32[]{:S(2)}, u32[]{:S(2)}) collective-permute-start(f32[2,16,63]{2,1,0:T(8,128)S(1)} %get-tuple-element.50), channel_id=1, source_target_pairs={{2,0},{4,2},{6,4},{8,6},{10,8},{12,10},{14,12},{3,1},{5,3},{7,5},{... | collective-permute-start | bytes 24200 | tf_op jit(solution)/shard_map/ppermute | solution.py:24
  198.0 29.2 %all-to-all-start.1 = ((f32[2,2,2,128,1,128]{5,2,0,1,4,3:T(2,128)}), f32[2,2,2,128,1,128]{5,2,0,1,4,3:T(2,128)S(1)}, u32[]{:S(2)}, u32[]{:S(2)}) async-start(f32[2,2,2,128,1,128]{5,2,0,1,4,3:T(2,128)} %copy.117), calls=%async_computation.1 | async-start | bytes 1048576 | tf_op jit(solution)/shard_map/all_to_all | solution.py:170
  231.7 15.0 %all-to-all-start.2 = ((f32[2,2,2,16,8,128]{5,3,1,0,2,4:T(8,128)}), f32[2,2,2,16,8,128]{5,3,1,0,2,4:T(8,128)S(1)}, u32[]{:S(2)}, u32[]{:S(2)}) async-start(f32[2,2,2,16,8,128]{5,3,1,0,2,4:T(8,128)} %copy.123), calls=%async_computation.2 | async-start | bytes 1048576 | tf_op jit(solution)/shard_map/all_to_all | solution.py:93
where the time goes:
time: 253 us; the launch traced here: 252 us
  local copies, waits for them, and re-layouts  181 us (72%)
  blocking collectives  22.1 us (9%)
  starting transfers between devices  19 us (8%)
  waiting for transfers between devices  13.8 us (5%)
  matrix products  10.2 us (4%)
  other arithmetic  4.66 us (2%)
    gather x384, local copies, waits for them, and re-layouts  169 us
    psum x1, blocking collectives, per_device(): totals = lax.psum(local_sums, ('tm', 'band'))  22.1 us
    all_to_all x1, waiting for transfers between devices, finish(): lax.all_to_all(packed, ('tm', 'band'), split_axis=4, concat_axis=3, tiled...  10.6 us
    all_to_all x1, starting transfers between devices, per_device(): lax.all_to_all(payload[:, :, :, :, None, :], ('tm', 'band'), split_axis=3...  5.76 us
    ppermute x2, starting transfers between devices, shifted(): return lax.ppermute(value, axis, pairs)  5.3 us
  transfers between devices with their start and end apart: 5, of which 2 were waited for; matrix products, arithmetic and copies ran while one was open for 3% of the time, Pallas kernels for 0%

commit v1 on v0

--- a/solution.py
+++ b/solution.py
@@ -1,8 +1,12 @@
+import functools
 import math
 
 import jax
 import jax.numpy as jnp
+import numpy as np
 from jax import lax
+from jax.experimental import pallas as pl
+from jax.experimental.pallas import tpu as pltpu
 from jax.sharding import PartitionSpec as P
 
 NB = 2048
@@ -195,7 +199,378 @@
     return f_stat[:, :, None, :]
 
 
+LANES = 128
+ROWS = 8
+HALO = 2
+
+
+def split_table(table):
+    high = table.astype(jnp.bfloat16)
+    low = (table - high.astype(np.float64)).astype(jnp.bfloat16)
+    return np.stack([high, low])
+
+
+def unit(product, modulus, sign):
+    angle = sign * 2.0 * np.pi / modulus * (product % modulus)
+    return np.cos(angle), np.sin(angle)
+
+
+def inverse_tables():
+    p_at = np.arange(NP)[:, None]
+    l_at = np.arange(NQ)[None, :]
+    twist = np.stack(unit(p_at * l_at, NB, 1.0)) / math.sqrt(NB)
+    real, imag = unit(np.arange(NQ)[:, None] * l_at, NQ, 1.0)
+    full = np.block([[real, -imag], [imag, real]])
+    return twist.astype(np.float32), split_table(full)
+
+
+def forward_table():
+    lane = np.arange(LANES)
+    bins = ROWS * (lane % NP) + lane // NP
+    real, imag = unit(np.arange(LANES)[:, None] * bins[None, :], LANES, -1.0)
+    return split_table(np.block([[real, imag], [-imag, real]]))
+
+
+def add(one, two):
+    return one[0] + two[0], one[1] + two[1]
+
+
+def sub(one, two):
+    return one[0] - two[0], one[1] - two[1]
+
+
+def turn(value, step, length, sign):
+    real, imag = value
+    step = step % length
+    if step == 0:
+        return value
+    if 2 * step == length:
+        return -real, -imag
+    if 4 * step == length:
+        return (-imag, real) if sign > 0 else (imag, -real)
+    if 4 * step == 3 * length:
+        return (imag, -real) if sign > 0 else (-imag, real)
+    angle = sign * 2.0 * math.pi * step / length
+    cos_part, sin_part = math.cos(angle), math.sin(angle)
+    if 8 * step == length:
+        root = math.sqrt(0.5)
+        if sign > 0:
+            return (real - imag) * root, (real + imag) * root
+        return (real + imag) * root, (imag - real) * root
+    return real * cos_part - imag * sin_part, real * sin_part + imag * cos_part
+
+
+def small_fft(values, sign):
+    length = len(values)
+    if length == 1:
+        return values
+    if length == 2:
+        return [add(values[0], values[1]), sub(values[0], values[1])]
+    even = small_fft(values[0::2], sign)
+    odd = small_fft(values[1::2], sign)
+    half = length // 2
+    turned = [turn(odd[k], k, length, sign) for k in range(half)]
+    return [add(even[k], turned[k]) for k in range(half)] + [sub(even[k], turned[k]) for k in range(half)]
+
+
+def times(value, cos_part, sin_part):
+    real, imag = value
+    return real * cos_part - imag * sin_part, real * sin_part + imag * cos_part
+
+
+def block_transpose(tile):
+    row = lax.broadcasted_iota(jnp.int32, (ROWS, LANES), 0)
+    group = lax.broadcasted_iota(jnp.int32, (ROWS, LANES), 1) // NP
+    for bit in (1, 2, 4):
+        row_bit = (row & bit) != 0
+        group_bit = (group & bit) != 0
+        up = pltpu.roll(pltpu.roll(tile, ROWS - bit, 0), NP * bit, 1)
+        if bit == 4:
+            moved = up
+        else:
+            down = pltpu.roll(pltpu.roll(tile, bit, 0), LANES - NP * bit, 1)
+            moved = jnp.where(group_bit, up, down)
+        tile = jnp.where(row_bit == group_bit, tile, moved)
+    return tile
+
+
+def split_dot(lhs, rhs, dims):
+    out = None
+    for one, two in ((0, 0), (0, 1), (1, 0)):
+        part = lax.dot_general(lhs[one], rhs[two], dims, preferred_element_type=jnp.float32)
+        out = part if out is None else out + part
+    return out
+
+
+def split_value(value):
+    high = value.astype(jnp.bfloat16)
+    return high, (value - high.astype(jnp.float32)).astype(jnp.bfloat16)
+
+
+def prepare_kernel(code_ref, antenna_ref, fraction_ref, weights_ref):
+    tmpl_local = code_ref.shape[0]
+    owners = weights_ref.shape[0]
+    stride = weights_ref.shape[1]
+    for t in range(tmpl_local):
+        for h in range(2):
+            for j in range(owners):
+                rows = pl.ds(2 * ROWS * j + ROWS * h, ROWS)
+                level = (code_ref[t, rows, :] & (NFRAC - 1)).astype(jnp.float32) * (1.0 / NFRAC)
+                fraction_ref[pl.ds(t * 128 + h * ROWS + j, ROWS, stride=2 * ROWS), :] = block_transpose(level)
+        sums = [jnp.zeros((ROWS, LANES), jnp.float32) for _ in range(3)]
+        for h in range(2):
+            for j in range(owners):
+                rows = pl.ds(2 * ROWS * j + ROWS * h, ROWS)
+                one = antenna_ref[t, 0, rows, :]
+                two = antenna_ref[t, 1, rows, :]
+                sums = [sums[0] + one * one, sums[1] + two * two, sums[2] + one * two]
+                for w, tile in ((0, one), (1, two)):
+                    weights_ref[j, pl.ds(t * 4 + w * 2 + h, ROWS, stride=ROWS), :] = block_transpose(tile)
+        for index in range(3):
+            row = jnp.sum(sums[index], axis=0, keepdims=True)
+            for j in range(owners):
+                weights_ref[j, pl.ds(stride - ROWS + t * 4 + index, 1), :] = row
+        for j in range(owners):
+            weights_ref[j, pl.ds(stride - ROWS + t * 4 + 3, 1), :] = jnp.zeros((1, LANES), jnp.float32)
+
+
+def resample_kernel(start_ref, bins_ref, fraction_ref, twist_ref, table_ref, out_ref, z_ref, grid_ref, time_ref, run_ref):
+    for g in range(2):
+        values = []
+        for kappa in range(NP):
+            rows, cols = pl.ds(ROWS * g, ROWS), pl.ds(LANES * kappa, LANES)
+            values.append((bins_ref[0, rows, cols], bins_ref[1, rows, cols]))
+        values = small_fft(values, 1.0)
+        for p in range(NP):
+            cos_part = twist_ref[0, pl.ds(p, 1), :]
+            sin_part = twist_ref[1, pl.ds(p, 1), :]
+            turned = times(values[p], cos_part, sin_part)
+            for part in range(2):
+                z_ref[part, pl.ds(LANES * g + p, ROWS, stride=NP), :] = turned[part]
+    dims = (((1,), (1,)), ((), ()))
+    grid_ref[...] = split_dot((table_ref[0], table_ref[1]), split_value(jnp.concatenate([z_ref[0], z_ref[1]], axis=1)), dims)
+    lane = lax.broadcasted_iota(jnp.int32, (ROWS, LANES), 1)
+    per_sft = NB // LANES
+    for part in range(2):
+        for r in range(per_sft):
+            tile = grid_ref[pl.ds(NQ * part + ROWS * r, ROWS), pl.ds(0, LANES)]
+            time_ref[pl.ds(2 * (per_sft + r) + part, ROWS, stride=2 * per_sft), :] = block_transpose(tile)
+        for r in range(per_sft // 2):
+            late = grid_ref[pl.ds(NQ * part + ROWS * (r + per_sft // 2), ROWS), pl.ds(LANES, LANES)]
+            early = grid_ref[pl.ds(NQ * part + ROWS * r, ROWS), pl.ds(LANES, LANES)]
+            tile = block_transpose(jnp.where(lane < NP, late, early))
+            time_ref[pl.ds(2 * (r + per_sft // 2) + part, 1), :] = tile[0:1]
+            time_ref[pl.ds(2 * (per_sft * (SFT_DEV + 1) + r) + part, 1), :] = tile[1:2]
+
+    def one_sft(at, carry):
+        for j in range(ROWS):
+            start = start_ref[at * ROWS + j]
+            shift = start & (LANES - 1)
+            tile = time_ref[pl.ds((start >> 7) * 2, ROWS), :]
+            tile = pltpu.roll(tile, (LANES - shift) & (LANES - 1), 1)
+            run_ref[pl.ds(ROWS * j, ROWS), :] = jnp.where(lane < LANES - shift, tile, pltpu.roll(tile, ROWS - 2, 0))
+        t, s_local = at >> 3, at & 7
+        coeffs = [lagrange(fraction_ref[pl.ds((at * 2 + h) * ROWS, ROWS), :]) for h in range(2)]
+        for part in range(2):
+            rows = [run_ref[pl.ds(2 * i + part, ROWS, stride=ROWS), :] for i in range(3)]
+            totals = [coeffs[h][0] * rows[h] for h in range(2)]
+            for k in range(1, 4):
+                rolled = [pltpu.roll(row, LANES - k, 1) for row in rows]
+                for h in range(2):
+                    tap = jnp.where(lane < LANES - k, rolled[h], rolled[h + 1])
+                    totals[h] = totals[h] + coeffs[h][k] * tap
+            for h in range(2):
+                out_ref[pl.ds(s_local * ROWS + t * 4 + part * 2 + h, ROWS, stride=8 * ROWS), :] = totals[h]
+        return carry
+
+    lax.fori_loop(0, start_ref.shape[0] // ROWS, one_sft, 0)
+
+
+def section_kernel(samples_ref, weights_ref, out_ref, sums_ref, mid_ref):
+    owners = samples_ref.shape[0]
+    row = lax.broadcasted_iota(jnp.int32, (ROWS, LANES), 0)
+    imag_row = (row & 2) != 0
+    for s_local in range(SFT_DEV):
+        values = []
+        for i in range(owners):
+            pair = samples_ref[i, pl.ds(ROWS * s_local, ROWS), :]
+            weight = weights_ref[i, pl.ds(ROWS * s_local, ROWS), :]
+            real = jnp.where(imag_row, pltpu.roll(pair, 2, 0), pair)
+            imag = jnp.where(imag_row, pair, pltpu.roll(pair, ROWS - 2, 0))
+            values.append((real * weight, imag * weight))
+        values = small_fft(values, -1.0)
+        for c in range(owners):
+            turned = turn(values[c], c * s_local, owners * SFT_DEV, -1.0)
+            for part in range(2):
+                mid_ref[part, pl.ds((c * SFT_DEV + s_local) * ROWS, ROWS), :] = turned[part]
+    for c in range(owners):
+        values = []
+        for s_local in range(SFT_DEV):
+            rows = pl.ds((c * SFT_DEV + s_local) * ROWS, ROWS)
+            values.append((mid_ref[0, rows, :], mid_ref[1, rows, :]))
+        values = small_fft(values, -1.0)
+        for d in range(SFT_DEV):
+            for part in range(2):
+                out_ref[c, pl.ds(part * ROWS * ROWS + d, ROWS, stride=ROWS), :] = values[d][part]
+    total = weights_ref[0, pl.ds(SFT_DEV * ROWS, ROWS), :]
+    for i in range(1, owners):
+        total = total + weights_ref[i, pl.ds(SFT_DEV * ROWS, ROWS), :]
+    sums_ref[...] = jnp.broadcast_to(jnp.sum(total, axis=1, keepdims=True), (ROWS, LANES))
+
+
+def statistic_kernel(sample_total, parts_ref, sums_ref, coarse_ref, fine_ref, table_ref, out_ref):
+    rhs = (table_ref[0], table_ref[1])
+    dims = (((1,), (0,)), ((), ()))
+    tmpl_local = out_ref.shape[0]
+    owners = parts_ref.shape[0]
+    for t in range(tmpl_local):
+        spectra = []
+        for w in range(2):
+            values = []
+            for rho in range(2 * owners):
+                j, h = rho // 2, rho % 2
+                base = (t * 4 + w * 2 + h) * ROWS
+                value = tuple(parts_ref[j, pl.ds(part * ROWS * ROWS + base, ROWS), :] for part in range(2))
+                rows = pl.ds(rho * ROWS, ROWS)
+                values.append(times(value, coarse_ref[0, rows, :], coarse_ref[1, rows, :]))
+            values = small_fft(values, -1.0)
+            values = [
+                times(values[a], fine_ref[0, pl.ds(a * ROWS, ROWS), :], fine_ref[1, pl.ds(a * ROWS, ROWS), :])
+                for a in range(2 * owners)
+            ]
+            real = jnp.concatenate([value[0] for value in values], axis=0)
+            imag = jnp.concatenate([value[1] for value in values], axis=0)
+            lhs = split_value(jnp.concatenate([real, imag], axis=1))
+            out = split_dot(lhs, rhs, dims)
+            spectra.append((out[:, :LANES], out[:, LANES:]))
+        (a_real, a_imag), (b_real, b_imag) = spectra
+        power_a = sums_ref[pl.ds(t * 4, 1), :] * (1.0 / sample_total) + stat_eps
+        power_b = sums_ref[pl.ds(t * 4 + 1, 1), :] * (1.0 / sample_total) + stat_eps
+        cross_ab = sums_ref[pl.ds(t * 4 + 2, 1), :] * (1.0 / sample_total)
+        det_floor = jnp.maximum(power_a * power_b - cross_ab * cross_ab, floor_share * power_a * power_b)
+        f_stat = (
+            (power_b / det_floor) * (a_real * a_real + a_imag * a_imag)
+            + (power_a / det_floor) * (b_real * b_real + b_imag * b_imag)
+            - (2.0 * cross_ab / det_floor) * (a_real * b_real + a_imag * b_imag)
+        )
+        for a in range(2 * owners):
+            tile = block_transpose(f_stat[a * ROWS : (a + 1) * ROWS])
+            out_ref[t, pl.ds(a, ROWS, stride=2 * owners), :] = tile
+
+
+def vmem():
+    return pl.BlockSpec(memory_space=pltpu.VMEM)
+
+
+def exchange_bins(sft_bins):
+    owner_count = lax.axis_size("tm") * lax.axis_size("band")
+    first = lax.axis_index("band") == 0
+    near = jnp.where(
+        first,
+        jnp.concatenate([sft_bins[:, SFT_DEV:], sft_bins[:, SFT_DEV - 1 : SFT_DEV]], axis=1),
+        sft_bins[:, : SFT_DEV + 1],
+    )
+    tail, head = sft_bins[:, -1:], sft_bins[:, :1]
+    same = jnp.where(first, tail, head)
+    other = jnp.where(first, head, tail)
+    axes = ("tm", "band")
+    straight, crossed = [], []
+    for rank in range(owner_count):
+        up = rank % 2 == 0
+        target = rank + 2 if up else rank - 2
+        if 0 <= target < owner_count:
+            straight.append((rank, target))
+        target = rank - 1 if up else rank + 1
+        if 0 <= target < owner_count:
+            crossed.append((rank, target))
+    near = lax.ppermute(near, "band", [(0, 1), (1, 0)])
+    same = lax.ppermute(same, axes, straight)
+    other = lax.ppermute(other, axes, crossed)
+    mine = jnp.where(first, sft_bins[:, :SFT_DEV], sft_bins[:, SFT_DEV:])
+    inner = jnp.where(first, sft_bins[:, SFT_DEV : SFT_DEV + 1], sft_bins[:, SFT_DEV - 1 : SFT_DEV])
+    my_halo = jnp.where(first, jnp.concatenate([same, inner], axis=1), jnp.concatenate([inner, same], axis=1))
+    far_inner = near[:, SFT_DEV:]
+    far_halo = jnp.where(
+        first, jnp.concatenate([other, far_inner], axis=1), jnp.concatenate([far_inner, other], axis=1)
+    )
+    blank = jnp.zeros((2, ROWS - HALO, sft_bins.shape[2]), jnp.float32)
+    my_rows = jnp.concatenate([mine, my_halo, blank], axis=1)
+    far_rows = jnp.concatenate([near[:, :SFT_DEV], far_halo, blank], axis=1)
+    return jnp.concatenate(
+        [jnp.where(first, my_rows, far_rows), jnp.where(first, far_rows, my_rows)], axis=2
+    )
+
+
+def run_device(sft_bins, delay_code, antenna):
+    axes = ("tm", "band")
+    owners = lax.axis_size("tm") * lax.axis_size("band")
+    my_rank = lax.axis_index("tm") * lax.axis_size("band") + lax.axis_index("band")
+    sample_total = SFT_DEV * owners * NB
+    tmpl_local = delay_code.shape[0]
+    run_count = SFT_DEV * NB // RUN
+    f32 = jnp.float32
+    bins = exchange_bins(sft_bins)
+    slot = SFT_DEV * ROWS
+    fraction, weights = pl.pallas_call(
+        prepare_kernel,
+        out_shape=(
+            jax.ShapeDtypeStruct((tmpl_local * SFT_DEV * 2 * ROWS, LANES), f32),
+            jax.ShapeDtypeStruct((owners, slot + ROWS, LANES), f32),
+        ),
+        in_specs=[vmem(), vmem()],
+        out_specs=(vmem(), vmem()),
+        name="prepare",
+    )(delay_code, antenna)
+    weights = lax.all_to_all(weights, axes, split_axis=0, concat_axis=0, tiled=True)
+    offsets = delay_code[:, :: RUN // NP, ::NP] // NFRAC - MAXD
+    offsets = offsets.transpose(0, 2, 1).reshape(tmpl_local, run_count)
+    starts = (jnp.arange(run_count, dtype=jnp.int32) * RUN)[None, :] + offsets + (NB - 1)
+    twist, inverse_table = inverse_tables()
+    samples = pl.pallas_call(
+        resample_kernel,
+        out_shape=jax.ShapeDtypeStruct((owners * slot, LANES), f32),
+        in_specs=[pl.BlockSpec(memory_space=pltpu.SMEM)] + [vmem()] * 4,
+        out_specs=vmem(),
+        scratch_shapes=[
+            pltpu.VMEM((2, 2 * LANES, LANES), f32),
+            pltpu.VMEM((2 * LANES, 2 * LANES), f32),
+            pltpu.VMEM((2 * (SFT_DEV + 2) * NB // LANES, LANES), f32),
+            pltpu.VMEM((ROWS * ROWS, LANES), f32),
+        ],
+        name="resample",
+    )(starts.reshape(-1), bins, fraction, jnp.asarray(twist), jnp.asarray(inverse_table))
+    samples = lax.all_to_all(samples.reshape(owners, slot, LANES), axes, split_axis=0, concat_axis=0, tiled=True)
+    parts, sums = pl.pallas_call(
+        section_kernel,
+        out_shape=(
+            jax.ShapeDtypeStruct((owners, 2 * slot, LANES), f32),
+            jax.ShapeDtypeStruct((ROWS, LANES), f32),
+        ),
+        in_specs=[vmem(), vmem()],
+        out_specs=(vmem(), vmem()),
+        scratch_shapes=[pltpu.VMEM((2, owners * slot, LANES), f32)],
+        name="section",
+    )(samples, weights)
+    parts = lax.all_to_all(parts, axes, split_axis=0, concat_axis=0, tiled=True)
+    row = lax.broadcasted_iota(jnp.int32, (2 * owners * ROWS, LANES), 0)
+    lane = lax.broadcasted_iota(jnp.int32, (2 * owners * ROWS, LANES), 1)
+    freq = my_rank + owners * (row % ROWS)
+    coarse = jnp.stack(phase_pair((row // ROWS) * freq, sample_total // LANES, -1.0))
+    fine = jnp.stack(phase_pair(lane * (freq + owners * SFT_DEV * (row // ROWS)), sample_total, -1.0))
+    fine = fine * (1.0 / math.sqrt(sample_total))
+    f_stat = pl.pallas_call(
+        functools.partial(statistic_kernel, sample_total),
+        out_shape=jax.ShapeDtypeStruct((tmpl_local, NQ, LANES), f32),
+        in_specs=[vmem()] * 5,
+        out_specs=vmem(),
+        name="statistic",
+    )(parts, sums, coarse, fine, jnp.asarray(forward_table()))
+    return f_stat[:, :, None, :]
+
+
 def solution(mesh):
+    owners = mesh.shape["tm"] * mesh.shape["band"]
+    one_run_each = NB // RUN == owners and mesh.shape["band"] == 2
     in_specs = (
         P(None, ("groups", "tm"), "band"),
         P(("groups", "tmpl"), None, ("tm", "band")),
@@ -203,5 +578,9 @@
     )
     out_specs = P(("groups", "tmpl"), None, ("tm", "band"), None)
     return jax.shard_map(
-        per_device, mesh=mesh, in_specs=in_specs, out_specs=out_specs, check_vma=False
-    )
+        run_device if one_run_each else per_device,
+        mesh=mesh,
+        in_specs=in_specs,
+        out_specs=out_specs,
+        check_vma=False,
+    )

time: 253 us -> 70.3 us (0.28)
  local copies, waits for them, and re-layouts: 181 us -> 2.16 us
  Pallas kernels: 0 us -> 19.7 us
  matrix products: 10.2 us -> 0 us
  blocking collectives: 22.1 us -> 13.9 us
  waiting for transfers between devices: 13.8 us -> 10.8 us
    gather x384 -> x0, local copies, waits for them, and re-layouts: 169 us -> none
    psum x1 -> x0, blocking collectives: 22.1 us -> none  [per_device(): totals = lax.psum(local_sums, ('tm', 'band'))]
    pallas_call x0 -> x4, Pallas kernels: none -> 19.7 us  [the longest x1 9.5 us: run_device(): pl.pallas_call(prepare_kernel, out_shape=(jax.ShapeDtypeStruct((tmpl_loca...]
    all_to_all x0 -> x1, blocking collectives: none -> 13.9 us  [run_device(): lax.all_to_all(samples.reshape(owners, slot, LANES), axes, split_axis=0,...]
    dot_general x24 -> x0, matrix products: 10.2 us -> none  [the longest x6 2.62 us: complex_einsum(): jnp.einsum(pattern, lhs_imag, rhs_imag, precision=high)]
    all_to_all x3 -> x2, starting transfers between devices: 13.7 us -> 9.71 us  [the longest x1 6.21 us: run_device(): lax.all_to_all(weights, axes, split_axis=0, concat_axis=0, tiled=True)]
    unnamed x3 -> x6, local copies, waits for them, and re-layouts: 4.44 us -> 0.83 us
    ppermute x2 -> x3, waiting for transfers between devices: 3.2 us -> 0.01 us  [the longest x1 0.01 us: exchange_bins(): same = lax.ppermute(same, axes, straight)]
  transfers between devices with their start and end apart: 5 -> 5, of which waited for: 2 -> 2; matrix products, arithmetic and copies ran while one was open for 3% -> 6% of each run, Pallas kernels for 0% -> 22%
where the time goes in v1:
time: 70.3 us; the launch traced here: 69.7 us
  Pallas kernels  19.7 us (28%)
  starting transfers between devices  18.1 us (26%)
  blocking collectives  13.9 us (20%)
  waiting for transfers between devices  10.8 us (15%)
  other arithmetic  4.76 us (7%)
  local copies, waits for them, and re-layouts  2.16 us (3%)
    all_to_all x1, blocking collectives, run_device(): lax.all_to_all(samples.reshape(owners, slot, LANES), axes, split_axis=0,...  13.9 us
    all_to_all x1, waiting for transfers between devices, run_device(): parts = lax.all_to_all(parts, axes, split_axis=0, concat_axis=0, tiled=True)  10.4 us
    pallas_call x1, Pallas kernels, run_device(): pl.pallas_call(prepare_kernel, out_shape=(jax.ShapeDtypeStruct((tmpl_loca...  9.5 us
    all_to_all x1, starting transfers between devices, run_device(): lax.all_to_all(weights, axes, split_axis=0, concat_axis=0, tiled=True)  6.21 us
    pallas_call x1, Pallas kernels, run_device(): pl.pallas_call(resample_kernel, out_shape=jax.ShapeDtypeStruct((owners *...  5.56 us
    ppermute x1, starting transfers between devices, exchange_bins(): same = lax.ppermute(same, axes, straight)  4.74 us
    all_to_all x1, starting transfers between devices, run_device(): parts = lax.all_to_all(parts, axes, split_axis=0, concat_axis=0, tiled=True)  3.49 us
    ppermute x1, starting transfers between devices, exchange_bins(): near = lax.ppermute(near, 'band', [(0, 1), (1, 0)])  3.03 us
  transfers between devices with their start and end apart: 5, of which 2 were waited for; matrix products, arithmetic and copies ran while one was open for 6% of the time, Pallas kernels for 22%

profile of v1, /device:TPU:0, one launch (start us, length us, event | category | flops | bytes accessed | tf_op | source)
XLA Modules:
  0.0 69.7 jit_solution(10376066988891020187)
XLA Ops:
  0.0 1.0 %broadcast_select_fusion.2 = (f32[2,1,1024]{2,1,0:T(1,128)S(1)}, f32[2,1,1024]{2,1,0:T(1,128)S(1)}, f32[2,1,1024]{2,1,0:T(1,128)S(1)}, f32[2,1,1024]{2,1,0:T(1,128)S(1)}) fusion(pred[]{:T(512)S(6)} %eq.7, f32[2,16,1024]{2,1,0:T(8,128)} %param.6), kind=kLoop, calls=%fused_computation.34 | loop fusion | flops 6144 | bytes 65537 | tf_op jit(solution)/shard_map/jit(_where)/select_n | solution.py:474
  1.0 0.0 copy-start.2
  1.0 0.9 %slice_select_fusion = (f32[2,8,1024]{2,1,0:T(8,128)S(1)}, f32[2,8,1024]{2,1,0:T(8,128)S(1)}) fusion(f32[2,16,1024]{2,1,0:T(8,128)} %param.6, pred[]{:T(512)S(6)} %eq.7), kind=kLoop, calls=%fused_computation.25 | loop fusion | flops 16384 | bytes 262145 | tf_op jit(solution)/shard_map/jit(_where)/select_n | solution.py:489
  1.9 0.0 copy-done.2
  2.0 3.0 %collective-permute-start.1 = (f32[2,9,1024]{2,1,0:T(8,128)S(1)}, f32[2,9,1024]{2,1,0:T(8,128)S(1)}, u32[]{:S(2)}, u32[]{:S(2)}) collective-permute-start(f32[2,9,1024]{2,1,0:T(8,128)S(1)} %maximum_select_fusion), channel_id=1, source_target_pairs={{0,2},{2,0},{1,3},{3,1},{4,6},{6,4},{5,7},{7,5},{8,10},{10,8},{9,1... | collective-permute-start | bytes 221192 | tf_op jit(solution)/shard_map/ppermute | solution.py:486
  5.0 0.6 collective-permute-start.2
  5.6 4.7 %collective-permute-start = (f32[2,1,1024]{2,1,0:T(1,128)S(1)}, f32[2,1,1024]{2,1,0:T(1,128)S(1)}, u32[]{:S(2)}, u32[]{:S(2)}) collective-permute-start(f32[2,1,1024]{2,1,0:T(1,128)S(1)} %get-tuple-element.17), channel_id=1, source_target_pairs={{0,4},{4,8},{6,2},{8,12},{10,6},{14,10},{1,5},{5,9},{7,3},{9,13},{... | collective-permute-start | bytes 24584 | tf_op jit(solution)/shard_map/ppermute | solution.py:487
  10.4 9.5 %prepare.1 = (f32[256,128]{1,0:T(8,128)}, f32[8,72,128]{2,1,0:T(8,128)}) custom-call(s32[2,128,128]{2,1,0:T(8,128)} %code_ref.1, f32[2,2,128,128]{3,2,1,0:T(8,128)} %antenna_ref.1), custom_call_target="tpu_custom_call" | custom-call | tf_op jit(solution)/shard_map/prepare/pallas_call | solution.py:514
  19.9 6.2 %all-to-all-start.1 = ((f32[8,72,128]{2,1,0:T(8,128)}), f32[8,72,128]{2,1,0:T(8,128)S(1)}, u32[]{:S(2)}, u32[]{:S(2)}) async-start(f32[8,72,128]{2,1,0:T(8,128)} %get-tuple-element.10), calls=%async_computation.1 | async-start | bytes 589824 | tf_op jit(solution)/shard_map/all_to_all | solution.py:524
  26.1 1.0 %slice.32 = s32[2,8,8]{2,1,0:T(8,128)S(1)} slice(s32[2,128,128]{2,1,0:T(8,128)} %code_ref.1), slice={[0:2:1], [0:128:16], [0:128:16]} | slice | bytes 1024 | tf_op jit(solution)/shard_map/slice | solution.py:525
  27.1 0.1 copy.7
  27.2 0.1 reshape.548
  27.3 0.1 add.102
  27.4 0.6 add_add_fusion.start_ref
  28.0 0.1 pad.17.clone
  28.0 0.0 collective-permute-done
  28.1 0.0 collective-permute-done.1
  28.1 0.0 collective-permute-done.2
  28.2 0.1 fusion.1
  28.3 0.7 %pad_maximum_fusion.bins_ref = f32[2,16,2048]{2,1,0:T(8,128)} fusion(f32[2,16,1024]{2,1,0:T(8,128)S(1)} %get-tuple-element.14, f32[2,16,1024]{2,1,0:T(8,128)S(1)} %get-tuple-element.13), kind=kLoop, calls=%fused_computation | loop fusion | flops 65536 | bytes 524288 | tf_op jit(solution)/shard_map/concatenate | solution.py:499
  29.0 5.6 %resample.1 = f32[512,128]{1,0:T(8,128)} custom-call(s32[128]{0:T(128)} %add_add_fusion.start_ref, f32[2,16,2048]{2,1,0:T(8,128)} %pad_maximum_fusion.bins_ref, f32[256,128]{1,0:T(8,128)} %get-tuple-element.9.fraction_ref, f32[2,16,128]{2,1,0:T(8,128)} %constant.102.clone.twist_ref, bf16[2,256,256]{2,1,0:T(8,128)(2,1)} %constant.103.clone.table_ref), custom_call_target="tpu_custom_call" | custom-call | tf_op jit(solution)/shard_map/resample/pallas_call | solution.py:529
  34.5 0.4 all-to-all-done.1.weights_ref
  34.9 0.0 copy-start.1
  34.9 13.9 %all_to_all.15.samples_ref = f32[8,64,128]{2,1,0:T(8,128)} all-to-all(f32[8,64,128]{2,1,0:T(8,128)} %bitcast.6), channel_id=1, replica_groups=mesh['groups'=2,'tm'=4,'band'=2,'tmpl'=2] {'tm','band'}, dimensions={0} | all-to-all | bytes 524288 | tf_op jit(solution)/shard_map/all_to_all | solution.py:542
  48.9 0.0 copy-done.1
  48.9 2.1 %section.1 = (f32[8,128,128]{2,1,0:T(8,128)}, f32[8,128]{1,0:T(8,128)}) custom-call(f32[8,64,128]{2,1,0:T(8,128)} %all_to_all.15.samples_ref, f32[8,72,128]{2,1,0:T(8,128)} %copy-done.1), custom_call_target="tpu_custom_call" | custom-call | tf_op jit(solution)/shard_map/section/pallas_call | solution.py:543
  51.0 3.5 %all-to-all-start.2 = ((f32[8,128,128]{2,1,0:T(8,128)}), f32[8,128,128]{2,1,0:T(8,128)S(1)}, u32[]{:S(2)}, u32[]{:S(2)}) async-start(f32[8,128,128]{2,1,0:T(8,128)} %get-tuple-element.11), calls=%async_computation.2 | async-start | bytes 1048576 | tf_op jit(solution)/shard_map/all_to_all | solution.py:554
  54.5 0.6 fusion.11
  55.2 0.7 %pad_maximum_fusion.1 = (f32[2,128,128]{2,1,0:T(8,128)}, f32[2,128,128]{2,1,0:T(8,128)}) fusion(f32[1,128,128]{2,1,0:T(8,128)S(1)} %get-tuple-element.24, f32[1,128,128]{2,1,0:T(8,128)S(1)} %get-tuple-element.23, f32[1,128,128]{2,1,0:T(8,128)S(1)} %get-tuple-element.22, f32[1,128,128]{2,1,0:T(8,128)S(1)} %get-tuple-element.21), kind=kLoop, calls=%fused_computation.4 | loop fusion | flops 98304 | bytes 524288 | tf_op jit(solution)/shard_map/stack | solution.py:558
  55.9 10.4 %all-to-all-done.2.parts_ref = f32[8,128,128]{2,1,0:T(8,128)S(1)} async-done(((f32[8,128,128]{2,1,0:T(8,128)}), f32[8,128,128]{2,1,0:T(8,128)S(1)}, u32[]{:S(2)}, u32[]{:S(2)}) %all-to-all-start.2) | async-done | bytes 524320 | tf_op jit(solution)/shard_map/all_to_all | solution.py:554
  66.3 0.0 copy-start
  66.3 0.8 %copy-done = f32[8,128,128]{2,1,0:T(8,128)} copy-done((f32[8,128,128]{2,1,0:T(8,128)}, f32[8,128,128]{2,1,0:T(8,128)S(1)}, u32[]{:S(2)}) %copy-start) | copy-done | bytes 524312
  67.1 2.6 %statistic.1 = f32[2,128,128]{2,1,0:T(8,128)} custom-call(f32[8,128,128]{2,1,0:T(8,128)} %copy-done, f32[8,128]{1,0:T(8,128)} %get-tuple-element.12.sums_ref, f32[2,128,128]{2,1,0:T(8,128)} %get-tuple-element.25.coarse_ref, f32[2,128,128]{2,1,0:T(8,128)} %get-tuple-element.26.fine_ref, bf16[2,256,256]{2,1,0:T(8,128)(2,1)} %constant.104.clone.table_ref), custom_call_target="tpu_custom_call" | custom-call | tf_op jit(solution)/shard_map/statistic/pallas_call | solution.py:561
  (15 shorter events, 0.1 us)
Async XLA Ops:
  1.0 1.0 %copy-start.2 = (f32[2,16,1024]{2,1,0:T(8,128)S(1)}, f32[2,16,1024]{2,1,0:T(8,128)}, u32[]{:S(2)}) copy-start(f32[2,16,1024]{2,1,0:T(8,128)} %param.6) | copy-start | bytes 393220
  2.0 26.1 %collective-permute-start.1 = (f32[2,9,1024]{2,1,0:T(8,128)S(1)}, f32[2,9,1024]{2,1,0:T(8,128)S(1)}, u32[]{:S(2)}, u32[]{:S(2)}) collective-permute-start(f32[2,9,1024]{2,1,0:T(8,128)S(1)} %maximum_select_fusion), channel_id=1, source_target_pairs={{0,2},{2,0},{1,3},{3,1},{4,6},{6,4},{5,7},{7,5},{8,10},{10,8},{9,1... | collective-permute-start | bytes 221192 | tf_op jit(solution)/shard_map/ppermute | solution.py:486
  5.0 23.1 %collective-permute-start.2 = (f32[2,1,1024]{2,1,0:T(1,128)S(1)}, f32[2,1,1024]{2,1,0:T(1,128)S(1)}, u32[]{:S(2)}, u32[]{:S(2)}) collective-permute-start(f32[2,1,1024]{2,1,0:T(1,128)S(1)} %get-tuple-element.20), channel_id=1, source_target_pairs={{2,4},{4,2},{6,8},{8,6},{10,12},{12,10},{3,5},{5,3},{7,9},{9,7},{1... | collective-permute-start | bytes 24584 | tf_op jit(solution)/shard_map/ppermute | solution.py:488
  5.6 22.4 %collective-permute-start = (f32[2,1,1024]{2,1,0:T(1,128)S(1)}, f32[2,1,1024]{2,1,0:T(1,128)S(1)}, u32[]{:S(2)}, u32[]{:S(2)}) collective-permute-start(f32[2,1,1024]{2,1,0:T(1,128)S(1)} %get-tuple-element.17), channel_id=1, source_target_pairs={{0,4},{4,8},{6,2},{8,12},{10,6},{14,10},{1,5},{5,9},{7,3},{9,13},{... | collective-permute-start | bytes 24584 | tf_op jit(solution)/shard_map/ppermute | solution.py:487
  19.9 15.1 %all-to-all-start.1 = ((f32[8,72,128]{2,1,0:T(8,128)}), f32[8,72,128]{2,1,0:T(8,128)S(1)}, u32[]{:S(2)}, u32[]{:S(2)}) async-start(f32[8,72,128]{2,1,0:T(8,128)} %get-tuple-element.10), calls=%async_computation.1 | async-start | bytes 589824 | tf_op jit(solution)/shard_map/all_to_all | solution.py:524
  34.9 13.9 %copy-start.1 = (f32[8,72,128]{2,1,0:T(8,128)}, f32[8,72,128]{2,1,0:T(8,128)S(1)}, u32[]{:S(2)}) copy-start(f32[8,72,128]{2,1,0:T(8,128)S(1)} %all-to-all-done.1.weights_ref) | copy-start | bytes 884740
  51.0 15.4 %all-to-all-start.2 = ((f32[8,128,128]{2,1,0:T(8,128)}), f32[8,128,128]{2,1,0:T(8,128)S(1)}, u32[]{:S(2)}, u32[]{:S(2)}) async-start(f32[8,128,128]{2,1,0:T(8,128)} %get-tuple-element.11), calls=%async_computation.2 | async-start | bytes 1048576 | tf_op jit(solution)/shard_map/all_to_all | solution.py:554
  66.3 0.8 %copy-start = (f32[8,128,128]{2,1,0:T(8,128)}, f32[8,128,128]{2,1,0:T(8,128)S(1)}, u32[]{:S(2)}) copy-start(f32[8,128,128]{2,1,0:T(8,128)S(1)} %all-to-all-done.2.parts_ref) | copy-start | bytes 1572868

commit v2 on v1

--- a/solution.py
+++ b/solution.py
@@ -278,20 +278,15 @@
     return real * cos_part - imag * sin_part, real * sin_part + imag * cos_part
 
 
-def block_transpose(tile):
+def block_transposes(tiles):
     row = lax.broadcasted_iota(jnp.int32, (ROWS, LANES), 0)
     group = lax.broadcasted_iota(jnp.int32, (ROWS, LANES), 1) // NP
-    for bit in (1, 2, 4):
-        row_bit = (row & bit) != 0
-        group_bit = (group & bit) != 0
-        up = pltpu.roll(pltpu.roll(tile, ROWS - bit, 0), NP * bit, 1)
-        if bit == 4:
-            moved = up
-        else:
-            down = pltpu.roll(pltpu.roll(tile, bit, 0), LANES - NP * bit, 1)
-            moved = jnp.where(group_bit, up, down)
-        tile = jnp.where(row_bit == group_bit, tile, moved)
-    return tile
+    gather_at = (group + row) & (ROWS - 1)
+    reverse_at = (ROWS - row) & (ROWS - 1)
+    tiles = [pltpu.roll(tile, 0, 1, stride=NP, stride_axis=0) for tile in tiles]
+    tiles = [jnp.take_along_axis(tile, gather_at, axis=0) for tile in tiles]
+    tiles = [pltpu.roll(tile, 0, 1, stride=NP, stride_axis=0) for tile in tiles]
+    return [jnp.take_along_axis(tile, reverse_at, axis=0) for tile in tiles]
 
 
 def split_dot(lhs, rhs, dims):
@@ -307,97 +302,171 @@
     return high, (value - high.astype(jnp.float32)).astype(jnp.bfloat16)
 
 
-def prepare_kernel(code_ref, antenna_ref, fraction_ref, weights_ref):
+def prepare_kernel(code_ref, antenna_ref, fraction_ref, weights_ref, sums_ref, start_ref):
     tmpl_local = code_ref.shape[0]
-    owners = weights_ref.shape[0]
-    stride = weights_ref.shape[1]
+    owners = code_ref.shape[1] // (2 * ROWS)
+    lane = lax.broadcasted_iota(jnp.int32, (ROWS, LANES), 1)
+    row = lax.broadcasted_iota(jnp.int32, (ROWS, LANES), 0)
     for t in range(tmpl_local):
         for h in range(2):
+            codes = [code_ref[t, pl.ds(2 * ROWS * j + ROWS * h, ROWS), :] for j in range(owners)]
+            turned = block_transposes(codes)
+            if h == 0:
+                starts = jnp.zeros((ROWS, LANES), jnp.int32)
+                for j in range(owners):
+                    starts = jnp.where(lane == j, jnp.broadcast_to(turned[j][:, 0:1], (ROWS, LANES)), starts)
+                starts = starts // NFRAC - MAXD + (row * owners + lane) * RUN + (NB - 1)
+                start_ref[pl.ds(t * ROWS, ROWS), :] = starts
             for j in range(owners):
-                rows = pl.ds(2 * ROWS * j + ROWS * h, ROWS)
-                level = (code_ref[t, rows, :] & (NFRAC - 1)).astype(jnp.float32) * (1.0 / NFRAC)
-                fraction_ref[pl.ds(t * 128 + h * ROWS + j, ROWS, stride=2 * ROWS), :] = block_transpose(level)
+                level = (turned[j] & (NFRAC - 1)).astype(jnp.float32) * (1.0 / NFRAC)
+                fraction_ref[pl.ds((t * SFT_DEV * 2 + h) * ROWS + j, ROWS, stride=2 * ROWS), :] = level
         sums = [jnp.zeros((ROWS, LANES), jnp.float32) for _ in range(3)]
         for h in range(2):
+            places = [pl.ds(2 * ROWS * j + ROWS * h, ROWS) for j in range(owners)]
+            one = [antenna_ref[t, 0, place, :] for place in places]
+            two = [antenna_ref[t, 1, place, :] for place in places]
+            for first, second in zip(one, two):
+                sums = [sums[0] + first * first, sums[1] + second * second, sums[2] + first * second]
+            for w, tiles in ((0, one), (1, two)):
+                turned = block_transposes(tiles)
+                for j in range(owners):
+                    at = ((t * 2 + w) * SFT_DEV * 2 + h) * ROWS + j
+                    weights_ref[pl.ds(at, ROWS, stride=2 * ROWS), :] = turned[j]
+        for index in range(3):
+            sums_ref[pl.ds(t * 4 + index, 1), :] = jnp.sum(sums[index], axis=0, keepdims=True)
+        sums_ref[pl.ds(t * 4 + 3, 1), :] = jnp.zeros((1, LANES), jnp.float32)
+
+
+def resample_kernel(
+    band_ref,
+    start_in_ref,
+    local_ref,
+    far_ref,
+    same_ref,
+    other_ref,
+    fraction_ref,
+    weights_ref,
+    sums_ref,
+    twist_ref,
+    table_ref,
+    out_ref,
+    z_ref,
+    grid_ref,
+    time_ref,
+    run_ref,
+    start_ref,
+    copy_sem,
+):
+    starts_copy = pltpu.make_async_copy(start_in_ref, start_ref, copy_sem)
+    starts_copy.start()
+    band = band_ref[0]
+    first = band == 0
+    half = NP // 2
+    owners = out_ref.shape[0]
+    slot = out_ref.shape[1]
+    tmpl_local = start_ref.shape[0] // SFT_DEV
+    row = lax.broadcasted_iota(jnp.int32, (ROWS, LANES), 0)
+    lane = lax.broadcasted_iota(jnp.int32, (ROWS, LANES), 1)
+    for group in range(2):
+        values = [[None, None] for _ in range(NP)]
+        for part in range(2):
+            for kappa in range(half):
+                cols = pl.ds(LANES * kappa, LANES)
+                if group == 0:
+                    rows = pl.ds(pl.multiple_of(band * SFT_DEV, SFT_DEV), SFT_DEV)
+                    mine = local_ref[part, rows, cols]
+                    far = far_ref[part, rows, cols]
+                else:
+                    inner = [
+                        jnp.where(first, ref[part, pl.ds(SFT_DEV, 1), cols], ref[part, pl.ds(SFT_DEV - 1, 1), cols])
+                        for ref in (local_ref, far_ref)
+                    ]
+                    mine = jnp.where(row == 0, same_ref[part, :, cols], inner[0])
+                    far = jnp.where(row == 0, other_ref[part, :, cols], inner[1])
+                values[kappa][part] = jnp.where(first, mine, far)
+                values[kappa + half][part] = jnp.where(first, far, mine)
+        values = small_fft([tuple(value) for value in values], 1.0)
+        for p in range(NP):
+            turned = times(values[p], twist_ref[0, pl.ds(p, 1), :], twist_ref[1, pl.ds(p, 1), :])
+            for part in range(2):
+                z_ref[part, pl.ds(LANES * group + p, ROWS, stride=NP), :] = turned[part]
+    dims = (((1,), (1,)), ((), ()))
+    z_value = split_value(jnp.concatenate([z_ref[0], z_ref[1]], axis=1))
+    grid_ref[...] = split_dot((table_ref[0], table_ref[1]), z_value, dims)
+    per_sft = NB // LANES
+    late_row = 2 * (per_sft // 2)
+    early_row = 2 * per_sft * (SFT_DEV + 1)
+    outer_row = jnp.where(first, late_row, early_row)
+    inner_row = jnp.where(first, early_row, late_row)
+    take_late = (lane < NP) == first
+    for part in range(2):
+        tiles = [grid_ref[pl.ds(NQ * part + ROWS * r, ROWS), pl.ds(0, LANES)] for r in range(per_sft)]
+        tiles = block_transposes(tiles)
+        for r in range(per_sft):
+            time_ref[pl.ds(2 * (per_sft + r) + part, ROWS, stride=2 * per_sft), :] = tiles[r]
+        tiles = [grid_ref[pl.ds(NQ * part + ROWS * r, ROWS), pl.ds(LANES, LANES)] for r in range(per_sft)]
+        tiles = [jnp.where(take_late, tiles[r + per_sft // 2], tiles[r]) for r in range(per_sft // 2)]
+        tiles = block_transposes(tiles)
+        for r in range(per_sft // 2):
+            time_ref[pl.ds(outer_row + 2 * r + part, 1), :] = tiles[r][0:1]
+            time_ref[pl.ds(inner_row + 2 * r + part, 1), :] = tiles[r][1:2]
+    for j in range(owners):
+        out_ref[j, pl.ds(slot - ROWS, ROWS), :] = sums_ref[...]
+    starts_copy.wait()
+    flat_ref = out_ref.reshape(owners * slot, LANES)
+
+    def one_sft(s_local, carry):
+        for t in range(tmpl_local):
+            starts = [start_ref[t * SFT_DEV + s_local, j] for j in range(owners)]
+            shifts = [start & (LANES - 1) for start in starts]
+            tiles = [time_ref[pl.ds((start >> 7) * 2, ROWS), :] for start in starts]
+            tiles = [pltpu.roll(tile, (LANES - shift) & (LANES - 1), 1) for tile, shift in zip(tiles, shifts)]
+            later = [pltpu.roll(tile, ROWS - 2, 0) for tile in tiles]
             for j in range(owners):
-                rows = pl.ds(2 * ROWS * j + ROWS * h, ROWS)
-                one = antenna_ref[t, 0, rows, :]
-                two = antenna_ref[t, 1, rows, :]
-                sums = [sums[0] + one * one, sums[1] + two * two, sums[2] + one * two]
-                for w, tile in ((0, one), (1, two)):
-                    weights_ref[j, pl.ds(t * 4 + w * 2 + h, ROWS, stride=ROWS), :] = block_transpose(tile)
-        for index in range(3):
-            row = jnp.sum(sums[index], axis=0, keepdims=True)
-            for j in range(owners):
-                weights_ref[j, pl.ds(stride - ROWS + t * 4 + index, 1), :] = row
-        for j in range(owners):
-            weights_ref[j, pl.ds(stride - ROWS + t * 4 + 3, 1), :] = jnp.zeros((1, LANES), jnp.float32)
-
-
-def resample_kernel(start_ref, bins_ref, fraction_ref, twist_ref, table_ref, out_ref, z_ref, grid_ref, time_ref, run_ref):
-    for g in range(2):
-        values = []
-        for kappa in range(NP):
-            rows, cols = pl.ds(ROWS * g, ROWS), pl.ds(LANES * kappa, LANES)
-            values.append((bins_ref[0, rows, cols], bins_ref[1, rows, cols]))
-        values = small_fft(values, 1.0)
-        for p in range(NP):
-            cos_part = twist_ref[0, pl.ds(p, 1), :]
-            sin_part = twist_ref[1, pl.ds(p, 1), :]
-            turned = times(values[p], cos_part, sin_part)
+                run_ref[pl.ds((t * owners + j) * ROWS, ROWS), :] = jnp.where(
+                    lane < LANES - shifts[j], tiles[j], later[j]
+                )
+        rows = [
+            [
+                [run_ref[pl.ds(t * owners * ROWS + 2 * i + part, ROWS, stride=ROWS), :] for i in range(3)]
+                for part in range(2)
+            ]
+            for t in range(tmpl_local)
+        ]
+        for t in range(tmpl_local):
+            at = (t * SFT_DEV + s_local) * 2
+            coeffs = [lagrange(fraction_ref[pl.ds((at + h) * ROWS, ROWS), :]) for h in range(2)]
+            weights = [
+                [
+                    weights_ref[pl.ds((((t * 2 + w) * SFT_DEV + s_local) * 2 + h) * ROWS, ROWS), :]
+                    for h in range(2)
+                ]
+                for w in range(2)
+            ]
             for part in range(2):
-                z_ref[part, pl.ds(LANES * g + p, ROWS, stride=NP), :] = turned[part]
-    dims = (((1,), (1,)), ((), ()))
-    grid_ref[...] = split_dot((table_ref[0], table_ref[1]), split_value(jnp.concatenate([z_ref[0], z_ref[1]], axis=1)), dims)
-    lane = lax.broadcasted_iota(jnp.int32, (ROWS, LANES), 1)
-    per_sft = NB // LANES
-    for part in range(2):
-        for r in range(per_sft):
-            tile = grid_ref[pl.ds(NQ * part + ROWS * r, ROWS), pl.ds(0, LANES)]
-            time_ref[pl.ds(2 * (per_sft + r) + part, ROWS, stride=2 * per_sft), :] = block_transpose(tile)
-        for r in range(per_sft // 2):
-            late = grid_ref[pl.ds(NQ * part + ROWS * (r + per_sft // 2), ROWS), pl.ds(LANES, LANES)]
-            early = grid_ref[pl.ds(NQ * part + ROWS * r, ROWS), pl.ds(LANES, LANES)]
-            tile = block_transpose(jnp.where(lane < NP, late, early))
-            time_ref[pl.ds(2 * (r + per_sft // 2) + part, 1), :] = tile[0:1]
-            time_ref[pl.ds(2 * (per_sft * (SFT_DEV + 1) + r) + part, 1), :] = tile[1:2]
-
-    def one_sft(at, carry):
-        for j in range(ROWS):
-            start = start_ref[at * ROWS + j]
-            shift = start & (LANES - 1)
-            tile = time_ref[pl.ds((start >> 7) * 2, ROWS), :]
-            tile = pltpu.roll(tile, (LANES - shift) & (LANES - 1), 1)
-            run_ref[pl.ds(ROWS * j, ROWS), :] = jnp.where(lane < LANES - shift, tile, pltpu.roll(tile, ROWS - 2, 0))
-        t, s_local = at >> 3, at & 7
-        coeffs = [lagrange(fraction_ref[pl.ds((at * 2 + h) * ROWS, ROWS), :]) for h in range(2)]
-        for part in range(2):
-            rows = [run_ref[pl.ds(2 * i + part, ROWS, stride=ROWS), :] for i in range(3)]
-            totals = [coeffs[h][0] * rows[h] for h in range(2)]
-            for k in range(1, 4):
-                rolled = [pltpu.roll(row, LANES - k, 1) for row in rows]
-                for h in range(2):
-                    tap = jnp.where(lane < LANES - k, rolled[h], rolled[h + 1])
-                    totals[h] = totals[h] + coeffs[h][k] * tap
-            for h in range(2):
-                out_ref[pl.ds(s_local * ROWS + t * 4 + part * 2 + h, ROWS, stride=8 * ROWS), :] = totals[h]
+                totals = [coeffs[h][0] * rows[t][part][h] for h in range(2)]
+                for k in range(1, 4):
+                    rolled = [pltpu.roll(tile, LANES - k, 1) for tile in rows[t][part]]
+                    for h in range(2):
+                        tap = jnp.where(lane < LANES - k, rolled[h], rolled[h + 1])
+                        totals[h] = totals[h] + coeffs[h][k] * tap
+                for w in range(2):
+                    for h in range(2):
+                        at = (part * SFT_DEV + s_local) * ROWS + t * 4 + w * 2 + h
+                        flat_ref[pl.ds(at, owners, stride=slot), :] = totals[h] * weights[w][h]
         return carry
 
-    lax.fori_loop(0, start_ref.shape[0] // ROWS, one_sft, 0)
-
-
-def section_kernel(samples_ref, weights_ref, out_ref, sums_ref, mid_ref):
+    lax.fori_loop(0, SFT_DEV, one_sft, 0)
+
+
+def section_kernel(samples_ref, out_ref, sums_ref, mid_ref):
     owners = samples_ref.shape[0]
-    row = lax.broadcasted_iota(jnp.int32, (ROWS, LANES), 0)
-    imag_row = (row & 2) != 0
+    slot = samples_ref.shape[1]
     for s_local in range(SFT_DEV):
-        values = []
-        for i in range(owners):
-            pair = samples_ref[i, pl.ds(ROWS * s_local, ROWS), :]
-            weight = weights_ref[i, pl.ds(ROWS * s_local, ROWS), :]
-            real = jnp.where(imag_row, pltpu.roll(pair, 2, 0), pair)
-            imag = jnp.where(imag_row, pair, pltpu.roll(pair, ROWS - 2, 0))
-            values.append((real * weight, imag * weight))
+        values = [
+            tuple(samples_ref[i, pl.ds((part * SFT_DEV + s_local) * ROWS, ROWS), :] for part in range(2))
+            for i in range(owners)
+        ]
         values = small_fft(values, -1.0)
         for c in range(owners):
             turned = turn(values[c], c * s_local, owners * SFT_DEV, -1.0)
@@ -412,9 +481,9 @@
         for d in range(SFT_DEV):
             for part in range(2):
                 out_ref[c, pl.ds(part * ROWS * ROWS + d, ROWS, stride=ROWS), :] = values[d][part]
-    total = weights_ref[0, pl.ds(SFT_DEV * ROWS, ROWS), :]
+    total = samples_ref[0, pl.ds(slot - ROWS, ROWS), :]
     for i in range(1, owners):
-        total = total + weights_ref[i, pl.ds(SFT_DEV * ROWS, ROWS), :]
+        total = total + samples_ref[i, pl.ds(slot - ROWS, ROWS), :]
     sums_ref[...] = jnp.broadcast_to(jnp.sum(total, axis=1, keepdims=True), (ROWS, LANES))
 
 
@@ -453,26 +522,22 @@
             + (power_a / det_floor) * (b_real * b_real + b_imag * b_imag)
             - (2.0 * cross_ab / det_floor) * (a_real * b_real + a_imag * b_imag)
         )
+        tiles = block_transposes([f_stat[a * ROWS : (a + 1) * ROWS] for a in range(2 * owners)])
         for a in range(2 * owners):
-            tile = block_transpose(f_stat[a * ROWS : (a + 1) * ROWS])
-            out_ref[t, pl.ds(a, ROWS, stride=2 * owners), :] = tile
+            out_ref[t, pl.ds(a, ROWS, stride=2 * owners), :] = tiles[a]
 
 
 def vmem():
     return pl.BlockSpec(memory_space=pltpu.VMEM)
+
+
+def resident(value):
+    return pltpu.with_memory_space_constraint(value, pltpu.VMEM)
 
 
 def exchange_bins(sft_bins):
     owner_count = lax.axis_size("tm") * lax.axis_size("band")
     first = lax.axis_index("band") == 0
-    near = jnp.where(
-        first,
-        jnp.concatenate([sft_bins[:, SFT_DEV:], sft_bins[:, SFT_DEV - 1 : SFT_DEV]], axis=1),
-        sft_bins[:, : SFT_DEV + 1],
-    )
-    tail, head = sft_bins[:, -1:], sft_bins[:, :1]
-    same = jnp.where(first, tail, head)
-    other = jnp.where(first, head, tail)
     axes = ("tm", "band")
     straight, crossed = [], []
     for rank in range(owner_count):
@@ -483,22 +548,11 @@
         target = rank - 1 if up else rank + 1
         if 0 <= target < owner_count:
             crossed.append((rank, target))
-    near = lax.ppermute(near, "band", [(0, 1), (1, 0)])
-    same = lax.ppermute(same, axes, straight)
-    other = lax.ppermute(other, axes, crossed)
-    mine = jnp.where(first, sft_bins[:, :SFT_DEV], sft_bins[:, SFT_DEV:])
-    inner = jnp.where(first, sft_bins[:, SFT_DEV : SFT_DEV + 1], sft_bins[:, SFT_DEV - 1 : SFT_DEV])
-    my_halo = jnp.where(first, jnp.concatenate([same, inner], axis=1), jnp.concatenate([inner, same], axis=1))
-    far_inner = near[:, SFT_DEV:]
-    far_halo = jnp.where(
-        first, jnp.concatenate([other, far_inner], axis=1), jnp.concatenate([far_inner, other], axis=1)
-    )
-    blank = jnp.zeros((2, ROWS - HALO, sft_bins.shape[2]), jnp.float32)
-    my_rows = jnp.concatenate([mine, my_halo, blank], axis=1)
-    far_rows = jnp.concatenate([near[:, :SFT_DEV], far_halo, blank], axis=1)
-    return jnp.concatenate(
-        [jnp.where(first, my_rows, far_rows), jnp.where(first, far_rows, my_rows)], axis=2
-    )
+    far = lax.ppermute(sft_bins, "band", [(0, 1), (1, 0)])
+    tail, head = sft_bins[:, -1:], sft_bins[:, :1]
+    same = lax.ppermute(jnp.where(first, tail, head), axes, straight)
+    other = lax.ppermute(jnp.where(first, head, tail), axes, crossed)
+    return far, same, other
 
 
 def run_device(sft_bins, delay_code, antenna):
@@ -507,50 +561,48 @@
     my_rank = lax.axis_index("tm") * lax.axis_size("band") + lax.axis_index("band")
     sample_total = SFT_DEV * owners * NB
     tmpl_local = delay_code.shape[0]
-    run_count = SFT_DEV * NB // RUN
     f32 = jnp.float32
-    bins = exchange_bins(sft_bins)
     slot = SFT_DEV * ROWS
-    fraction, weights = pl.pallas_call(
+    far, same, other = exchange_bins(sft_bins)
+    fraction, weights, sums, starts = pl.pallas_call(
         prepare_kernel,
         out_shape=(
-            jax.ShapeDtypeStruct((tmpl_local * SFT_DEV * 2 * ROWS, LANES), f32),
-            jax.ShapeDtypeStruct((owners, slot + ROWS, LANES), f32),
+            pltpu.VMEM((tmpl_local * SFT_DEV * 2 * ROWS, LANES), f32),
+            pltpu.VMEM((tmpl_local * 2 * SFT_DEV * 2 * ROWS, LANES), f32),
+            pltpu.VMEM((ROWS, LANES), f32),
+            pltpu.VMEM((tmpl_local * SFT_DEV, LANES), jnp.int32),
         ),
         in_specs=[vmem(), vmem()],
-        out_specs=(vmem(), vmem()),
+        out_specs=(vmem(),) * 4,
         name="prepare",
-    )(delay_code, antenna)
-    weights = lax.all_to_all(weights, axes, split_axis=0, concat_axis=0, tiled=True)
-    offsets = delay_code[:, :: RUN // NP, ::NP] // NFRAC - MAXD
-    offsets = offsets.transpose(0, 2, 1).reshape(tmpl_local, run_count)
-    starts = (jnp.arange(run_count, dtype=jnp.int32) * RUN)[None, :] + offsets + (NB - 1)
+    )(resident(delay_code), resident(antenna))
     twist, inverse_table = inverse_tables()
+    band = lax.axis_index("band").astype(jnp.int32).reshape(1)
+    operands = [starts, sft_bins, far, same, other, fraction, weights, sums, jnp.asarray(twist), jnp.asarray(inverse_table)]
     samples = pl.pallas_call(
         resample_kernel,
-        out_shape=jax.ShapeDtypeStruct((owners * slot, LANES), f32),
-        in_specs=[pl.BlockSpec(memory_space=pltpu.SMEM)] + [vmem()] * 4,
+        out_shape=pltpu.VMEM((owners, 2 * slot + ROWS, LANES), f32),
+        in_specs=[pl.BlockSpec(memory_space=pltpu.SMEM)] + [vmem()] * len(operands),
         out_specs=vmem(),
         scratch_shapes=[
             pltpu.VMEM((2, 2 * LANES, LANES), f32),
             pltpu.VMEM((2 * LANES, 2 * LANES), f32),
             pltpu.VMEM((2 * (SFT_DEV + 2) * NB // LANES, LANES), f32),
-            pltpu.VMEM((ROWS * ROWS, LANES), f32),
+            pltpu.VMEM((tmpl_local * owners * ROWS, LANES), f32),
+            pltpu.SMEM((tmpl_local * SFT_DEV, LANES), jnp.int32),
+            pltpu.SemaphoreType.DMA,
         ],
         name="resample",
-    )(starts.reshape(-1), bins, fraction, jnp.asarray(twist), jnp.asarray(inverse_table))
-    samples = lax.all_to_all(samples.reshape(owners, slot, LANES), axes, split_axis=0, concat_axis=0, tiled=True)
-    parts, sums = pl.pallas_call(
+    )(band, *[resident(operand) for operand in operands])
+    samples = lax.all_to_all(samples, axes, split_axis=0, concat_axis=0, tiled=True)
+    parts, totals = pl.pallas_call(
         section_kernel,
-        out_shape=(
-            jax.ShapeDtypeStruct((owners, 2 * slot, LANES), f32),
-            jax.ShapeDtypeStruct((ROWS, LANES), f32),
-        ),
-        in_specs=[vmem(), vmem()],
+        out_shape=(pltpu.VMEM((owners, 2 * slot, LANES), f32), pltpu.VMEM((ROWS, LANES), f32)),
+        in_specs=[vmem()],
         out_specs=(vmem(), vmem()),
         scratch_shapes=[pltpu.VMEM((2, owners * slot, LANES), f32)],
         name="section",
-    )(samples, weights)
+    )(resident(samples))
     parts = lax.all_to_all(parts, axes, split_axis=0, concat_axis=0, tiled=True)
     row = lax.broadcasted_iota(jnp.int32, (2 * owners * ROWS, LANES), 0)
     lane = lax.broadcasted_iota(jnp.int32, (2 * owners * ROWS, LANES), 1)
@@ -558,13 +610,14 @@
     coarse = jnp.stack(phase_pair((row // ROWS) * freq, sample_total // LANES, -1.0))
     fine = jnp.stack(phase_pair(lane * (freq + owners * SFT_DEV * (row // ROWS)), sample_total, -1.0))
     fine = fine * (1.0 / math.sqrt(sample_total))
+    operands = [parts, totals, coarse, fine, jnp.asarray(forward_table())]
     f_stat = pl.pallas_call(
         functools.partial(statistic_kernel, sample_total),
         out_shape=jax.ShapeDtypeStruct((tmpl_local, NQ, LANES), f32),
-        in_specs=[vmem()] * 5,
+        in_specs=[vmem()] * len(operands),
         out_specs=vmem(),
         name="statistic",
-    )(parts, sums, coarse, fine, jnp.asarray(forward_table()))
+    )(*[resident(operand) for operand in operands])
     return f_stat[:, :, None, :]
 
 

time: 70.3 us -> 54.3 us (0.77)
  Pallas kernels: 19.7 us -> 5.25 us
  blocking collectives: 13.9 us -> 21.5 us
  starting transfers between devices: 18.1 us -> 10.6 us
  other arithmetic: 4.76 us -> 1.61 us
  waiting for transfers between devices: 10.8 us -> 12.7 us
    pallas_call x3, Pallas kernels: 17.1 us -> 3.95 us  [the longest x1 2.33 us: run_device(): pl.pallas_call(resample_kernel, out_shape=pltpu.VMEM((owners, 2 * slot +...]
    all_to_all x1, blocking collectives: 13.9 us -> 21.5 us  [run_device(): lax.all_to_all(samples, axes, split_axis=0, concat_axis=0, tiled=True)]
    all_to_all x1 -> x0, starting transfers between devices: 6.21 us -> none  [run_device(): lax.all_to_all(weights, axes, split_axis=0, concat_axis=0, tiled=True)]
    all_to_all x1, waiting for transfers between devices: 10.4 us -> 12.7 us  [run_device(): parts = lax.all_to_all(parts, axes, split_axis=0, concat_axis=0, tiled=True)]
    unnamed x6 -> x12, local copies, waits for them, and re-layouts: 0.83 us -> 2.15 us
    ppermute x3, starting transfers between devices: 8.42 us -> 7.11 us  [the longest x1 3.48 us: exchange_bins(): same = lax.ppermute(jnp.where(first, tail, head), axes, straight)]
    pallas_call x1, Pallas kernels: 2.56 us -> 1.3 us  [run_device(): pl.pallas_call(functools.partial(statistic_kernel, sample_total), out_sha...]
    select_n x6 -> x1, other arithmetic: 2.05 us -> 0.92 us  [exchange_bins(): other = lax.ppermute(jnp.where(first, head, tail), axes, crossed)]
  transfers between devices with their start and end apart: 5 -> 4, of which waited for: 2 -> 1; matrix products, arithmetic and copies ran while one was open for 6% -> 3% of each run, Pallas kernels for 22% -> 1%
where the time goes in v2:
time: 54.3 us; the launch traced here: 53.9 us
  blocking collectives  21.5 us (40%)
  waiting for transfers between devices  12.7 us (23%)
  starting transfers between devices  10.6 us (20%)
  Pallas kernels  5.25 us (10%)
  local copies, waits for them, and re-layouts  2.15 us (4%)
  other arithmetic  1.61 us (3%)
    all_to_all x1, blocking collectives, run_device(): lax.all_to_all(samples, axes, split_axis=0, concat_axis=0, tiled=True)  21.5 us
    all_to_all x1, waiting for transfers between devices, run_device(): parts = lax.all_to_all(parts, axes, split_axis=0, concat_axis=0, tiled=True)  12.7 us
    all_to_all x1, starting transfers between devices, run_device(): parts = lax.all_to_all(parts, axes, split_axis=0, concat_axis=0, tiled=True)  3.49 us
    ppermute x1, starting transfers between devices, exchange_bins(): same = lax.ppermute(jnp.where(first, tail, head), axes, straight)  3.48 us
    ppermute x1, starting transfers between devices, exchange_bins(): far = lax.ppermute(sft_bins, 'band', [(0, 1), (1, 0)])  2.97 us
    pallas_call x1, Pallas kernels, run_device(): pl.pallas_call(resample_kernel, out_shape=pltpu.VMEM((owners, 2 * slot +...  2.33 us
    unnamed x12, local copies, waits for them, and re-layouts  2.15 us
    pallas_call x1, Pallas kernels, run_device(): pl.pallas_call(functools.partial(statistic_kernel, sample_total), out_sha...  1.3 us
  transfers between devices with their start and end apart: 4, of which 1 were waited for; matrix products, arithmetic and copies ran while one was open for 3% of the time, Pallas kernels for 1%

profile of v2, /device:TPU:0, one launch (start us, length us, event | category | flops | bytes accessed | tf_op | source)
XLA Modules:
  0.0 53.9 jit_solution(12130503959655174622)
XLA Ops:
  0.0 3.0 %collective-permute-start = (f32[2,16,1024]{2,1,0:T(8,128)}, f32[2,16,1024]{2,1,0:T(8,128)S(1)}, u32[]{:S(2)}, u32[]{:S(2)}) collective-permute-start(f32[2,16,1024]{2,1,0:T(8,128)} %local_ref.1), channel_id=1, source_target_pairs={{0,2},{2,0},{1,3},{3,1},{4,6},{6,4},{5,7},{7,5},{8,10},{10,8},{9,1... | collective-permute-start | bytes 393224 | tf_op jit(solution)/shard_map/ppermute | solution.py:551
  3.0 0.0 copy-start.5
  3.0 0.9 %broadcast_select_fusion = (f32[2,1,1024]{2,1,0:T(1,128)S(1)}, f32[2,1,1024]{2,1,0:T(1,128)S(1)}) fusion(pred[]{:T(512)S(6)} %eq.7, f32[2,16,1024]{2,1,0:T(8,128)} %local_ref.1), kind=kLoop, calls=%fused_computation.23 | loop fusion | flops 4096 | bytes 32769 | tf_op jit(solution)/shard_map/jit(_where)/select_n | solution.py:554
  3.9 3.5 %collective-permute-start.1 = (f32[2,1,1024]{2,1,0:T(1,128)S(1)}, f32[2,1,1024]{2,1,0:T(1,128)S(1)}, u32[]{:S(2)}, u32[]{:S(2)}) collective-permute-start(f32[2,1,1024]{2,1,0:T(1,128)S(1)} %get-tuple-element.18), channel_id=1, source_target_pairs={{0,4},{4,8},{6,2},{8,12},{10,6},{14,10},{1,5},{5,9},{7,3},{9,13},{... | collective-permute-start | bytes 24584 | tf_op jit(solution)/shard_map/ppermute | solution.py:553
  7.4 0.7 %collective-permute-start.2 = (f32[2,1,1024]{2,1,0:T(1,128)S(1)}, f32[2,1,1024]{2,1,0:T(1,128)S(1)}, u32[]{:S(2)}, u32[]{:S(2)}) collective-permute-start(f32[2,1,1024]{2,1,0:T(1,128)S(1)} %get-tuple-element.17), channel_id=1, source_target_pairs={{2,4},{4,2},{6,8},{8,6},{10,12},{12,10},{3,5},{5,3},{7,9},{9,7},{1... | collective-permute-start | bytes 24584 | tf_op jit(solution)/shard_map/ppermute | solution.py:554
  8.1 0.0 copy-start
  8.1 0.9 %copy-done = f32[2,2,128,128]{3,2,1,0:T(8,128)S(1)} copy-done((f32[2,2,128,128]{3,2,1,0:T(8,128)S(1)}, f32[2,2,128,128]{3,2,1,0:T(8,128)}, u32[]{:S(2)}) %copy-start) | copy-done | bytes 262168
  9.0 0.0 copy-start.4
  9.0 0.9 %copy-done.4 = s32[2,128,128]{2,1,0:T(8,128)S(1)} copy-done((s32[2,128,128]{2,1,0:T(8,128)S(1)}, s32[2,128,128]{2,1,0:T(8,128)}, u32[]{:S(2)}) %copy-start.4) | copy-done | bytes 131096
  9.9 0.0 copy-start.2
  9.9 0.0 copy-start.3
  9.9 0.6 %prepare.1 = (f32[256,128]{1,0:T(8,128)S(1)}, f32[512,128]{1,0:T(8,128)S(1)}, f32[8,128]{1,0:T(8,128)S(1)}, s32[16,128]{1,0:T(8,128)S(1)}) custom-call(s32[2,128,128]{2,1,0:T(8,128)S(1)} %copy-done.4, f32[2,2,128,128]{3,2,1,0:T(8,128)S(1)} %copy-done), custom_call_target="tpu_custom_call" | custom-call | tf_op jit(solution)/shard_map/prepare/pallas_call | solution.py:567
  10.6 0.0 collective-permute-done.1.same_ref
  10.6 0.0 collective-permute-done.2.other_ref
  10.6 0.0 collective-permute-done.far_ref
  10.6 0.0 copy-done.5
  10.6 0.3 copy-done.2
  10.9 0.0 copy-done.3
  10.9 2.3 %resample.1 = f32[8,136,128]{2,1,0:T(8,128)S(1)} custom-call(s32[1]{0:T(128)} %bitcast.band_ref, s32[16,128]{1,0:T(8,128)S(1)} %get-tuple-element.11.start_in_ref, f32[2,16,1024]{2,1,0:T(8,128)S(1)} %copy-done.3, f32[2,16,1024]{2,1,0:T(8,128)S(1)} %collective-permute-done.far_ref, f32[2,1,1024]{2,1,0:T(1,128)S(1)} %collective-permute-done.1.same_ref, ...), custom_call_target="tpu_custom_call" | custom-call | tf_op jit(solution)/shard_map/resample/pallas_call | solution.py:582
  13.2 21.5 %all_to_all.10.samples_ref = f32[8,136,128]{2,1,0:T(8,128)S(1)} all-to-all(f32[8,136,128]{2,1,0:T(8,128)S(1)} %resample.1), channel_id=1, replica_groups=mesh['groups'=2,'tm'=4,'band'=2,'tmpl'=2] {'tm','band'}, dimensions={0} | all-to-all | bytes 1114112 | tf_op jit(solution)/shard_map/all_to_all | solution.py:597
  34.7 1.0 %section.1 = (f32[8,128,128]{2,1,0:T(8,128)}, f32[8,128]{1,0:T(8,128)S(1)}) custom-call(f32[8,136,128]{2,1,0:T(8,128)S(1)} %all_to_all.10.samples_ref), custom_call_target="tpu_custom_call" | custom-call | tf_op jit(solution)/shard_map/section/pallas_call | solution.py:598
  35.7 3.5 %all-to-all-start.1 = ((f32[8,128,128]{2,1,0:T(8,128)}), f32[8,128,128]{2,1,0:T(8,128)S(1)}, u32[]{:S(2)}, u32[]{:S(2)}) async-start(f32[8,128,128]{2,1,0:T(8,128)} %get-tuple-element.15), calls=%async_computation.1 | async-start | bytes 1048576 | tf_op jit(solution)/shard_map/all_to_all | solution.py:606
  39.3 0.6 %fusion.9 = (f32[1,128,128]{2,1,0:T(8,128)S(1)}, f32[1,128,128]{2,1,0:T(8,128)S(1)}, f32[1,128,128]{2,1,0:T(8,128)S(1)}, f32[1,128,128]{2,1,0:T(8,128)S(1)}) fusion(s32[128]{0:T(128)S(1)} %iota_shift-right-logical_fusion, s32[128]{0:T(128)S(1)} %broadcast_add_fusion.1, pred[128]{0:T(512)(128)(4,1)S(1)} %compare_and_fusion.1, s32[128]{0:T(128)S(1)} %iota_and_fusion, ...), kind=kLoop, calls=%fused_computation.20 | loop fusion | flops 557056 | bytes 264452 | tf_op jit(solution)/shard_map/cos | solution.py:42
  39.9 0.0 copy-start.1
  40.0 12.7 %all-to-all-done.1.parts_ref = f32[8,128,128]{2,1,0:T(8,128)S(1)} async-done(((f32[8,128,128]{2,1,0:T(8,128)}), f32[8,128,128]{2,1,0:T(8,128)S(1)}, u32[]{:S(2)}, u32[]{:S(2)}) %all-to-all-start.1) | async-done | bytes 524320 | tf_op jit(solution)/shard_map/all_to_all | solution.py:606
  52.6 0.0 copy-done.1
  52.6 1.3 %statistic.1 = f32[2,128,128]{2,1,0:T(8,128)} custom-call(f32[8,128,128]{2,1,0:T(8,128)S(1)} %all-to-all-done.1.parts_ref, f32[8,128]{1,0:T(8,128)S(1)} %get-tuple-element.16.sums_ref, f32[2,128,128]{2,1,0:T(8,128)S(1)} %get-tuple-element.23.coarse_ref, f32[2,128,128]{2,1,0:T(8,128)S(1)} %get-tuple-element.24.fine_ref, bf16[2,256,256]{2,1,0:T(8,128)(2,1)S(1)} %copy-done.1), custom_call_target="tpu_custom_call" | custom-call | tf_op jit(solution)/shard_map/statistic/pallas_call | solution.py:614
  (7 shorter events, 0.0 us)
Async XLA Ops:
  0.0 10.6 %collective-permute-start = (f32[2,16,1024]{2,1,0:T(8,128)}, f32[2,16,1024]{2,1,0:T(8,128)S(1)}, u32[]{:S(2)}, u32[]{:S(2)}) collective-permute-start(f32[2,16,1024]{2,1,0:T(8,128)} %local_ref.1), channel_id=1, source_target_pairs={{0,2},{2,0},{1,3},{3,1},{4,6},{6,4},{5,7},{7,5},{8,10},{10,8},{9,1... | collective-permute-start | bytes 393224 | tf_op jit(solution)/shard_map/ppermute | solution.py:551
  3.0 7.6 %copy-start.5 = (f32[2,16,128]{2,1,0:T(8,128)S(1)}, f32[2,16,128]{2,1,0:T(8,128)}, u32[]{:S(2)}) copy-start(f32[2,16,128]{2,1,0:T(8,128)} %constant.84.clone.twist_ref) | copy-start | bytes 49156
  3.9 6.7 %collective-permute-start.1 = (f32[2,1,1024]{2,1,0:T(1,128)S(1)}, f32[2,1,1024]{2,1,0:T(1,128)S(1)}, u32[]{:S(2)}, u32[]{:S(2)}) collective-permute-start(f32[2,1,1024]{2,1,0:T(1,128)S(1)} %get-tuple-element.18), channel_id=1, source_target_pairs={{0,4},{4,8},{6,2},{8,12},{10,6},{14,10},{1,5},{5,9},{7,3},{9,13},{... | collective-permute-start | bytes 24584 | tf_op jit(solution)/shard_map/ppermute | solution.py:553
  7.4 3.2 %collective-permute-start.2 = (f32[2,1,1024]{2,1,0:T(1,128)S(1)}, f32[2,1,1024]{2,1,0:T(1,128)S(1)}, u32[]{:S(2)}, u32[]{:S(2)}) collective-permute-start(f32[2,1,1024]{2,1,0:T(1,128)S(1)} %get-tuple-element.17), channel_id=1, source_target_pairs={{2,4},{4,2},{6,8},{8,6},{10,12},{12,10},{3,5},{5,3},{7,9},{9,7},{1... | collective-permute-start | bytes 24584 | tf_op jit(solution)/shard_map/ppermute | solution.py:554
  8.1 1.0 %copy-start = (f32[2,2,128,128]{3,2,1,0:T(8,128)S(1)}, f32[2,2,128,128]{3,2,1,0:T(8,128)}, u32[]{:S(2)}) copy-start(f32[2,2,128,128]{3,2,1,0:T(8,128)} %antenna_ref.1) | copy-start | bytes 786436
  9.0 0.9 %copy-start.4 = (s32[2,128,128]{2,1,0:T(8,128)S(1)}, s32[2,128,128]{2,1,0:T(8,128)}, u32[]{:S(2)}) copy-start(s32[2,128,128]{2,1,0:T(8,128)} %code_ref.1) | copy-start | bytes 393220
  9.9 0.9 %copy-start.2 = (bf16[2,256,256]{2,1,0:T(8,128)(2,1)S(1)}, bf16[2,256,256]{2,1,0:T(8,128)(2,1)}, u32[]{:S(2)}) copy-start(bf16[2,256,256]{2,1,0:T(8,128)(2,1)} %constant.85.clone.table_ref) | copy-start | bytes 786436
  9.9 1.0 %copy-start.3 = (f32[2,16,1024]{2,1,0:T(8,128)S(1)}, f32[2,16,1024]{2,1,0:T(8,128)}, u32[]{:S(2)}) copy-start(f32[2,16,1024]{2,1,0:T(8,128)} %local_ref.1) | copy-start | bytes 393220
  35.7 16.9 %all-to-all-start.1 = ((f32[8,128,128]{2,1,0:T(8,128)}), f32[8,128,128]{2,1,0:T(8,128)S(1)}, u32[]{:S(2)}, u32[]{:S(2)}) async-start(f32[8,128,128]{2,1,0:T(8,128)} %get-tuple-element.15), calls=%async_computation.1 | async-start | bytes 1048576 | tf_op jit(solution)/shard_map/all_to_all | solution.py:606
  39.9 12.7 %copy-start.1 = (bf16[2,256,256]{2,1,0:T(8,128)(2,1)S(1)}, bf16[2,256,256]{2,1,0:T(8,128)(2,1)}, u32[]{:S(2)}) copy-start(bf16[2,256,256]{2,1,0:T(8,128)(2,1)} %constant.86.clone.table_ref) | copy-start | bytes 786436

commit v3 on v2

--- a/solution.py
+++ b/solution.py
@@ -302,7 +302,8 @@
     return high, (value - high.astype(jnp.float32)).astype(jnp.bfloat16)
 
 
-def prepare_kernel(code_ref, antenna_ref, fraction_ref, weights_ref, sums_ref, start_ref):
+def prepare_kernel(code_ref, antenna_ref, bins_ref, fraction_ref, weights_ref, sums_ref, start_ref, mine_ref):
+    mine_ref[...] = bins_ref[...]
     tmpl_local = code_ref.shape[0]
     owners = code_ref.shape[1] // (2 * ROWS)
     lane = lax.broadcasted_iota(jnp.int32, (ROWS, LANES), 1)
@@ -337,13 +338,89 @@
         sums_ref[pl.ds(t * 4 + 3, 1), :] = jnp.zeros((1, LANES), jnp.float32)
 
 
+def pack_kernel(band_ref, mine_ref, far_ref, out_ref):
+    first = band_ref[0] == 0
+    half = NP // 2
+    last = mine_ref.shape[1] - 1
+    for part in range(2):
+        for kappa in range(half):
+            cols = pl.ds(LANES * kappa, LANES)
+            mine, far = [
+                jnp.where(first, ref[part, pl.ds(last, 1), cols], ref[part, pl.ds(0, 1), cols])
+                for ref in (mine_ref, far_ref)
+            ]
+            out_ref[part, pl.ds(kappa, 1), :] = jnp.where(first, mine, far)
+            out_ref[part, pl.ds(kappa + half, 1), :] = jnp.where(first, far, mine)
+
+
+def inverse_columns(values, twist_ref, z_ref, places):
+    values = small_fft(values, 1.0)
+    for p in range(NP):
+        turned = times(values[p], twist_ref[0, pl.ds(p, 1), :], twist_ref[1, pl.ds(p, 1), :])
+        for part in range(2):
+            z_ref[part, places[p], :] = turned[part]
+
+
+def inverse_grid(table_ref, z_ref):
+    z_value = split_value(jnp.concatenate([z_ref[0], z_ref[1]], axis=1))
+    return split_dot((table_ref[0], table_ref[1]), z_value, (((1,), (1,)), ((), ())))
+
+
+def halo_rows(grid, part, late):
+    per_sft = NB // LANES
+    tiles = [grid[NQ * part + ROWS * r : NQ * part + ROWS * (r + 1)] for r in range(per_sft)]
+    tiles = [jnp.where(late, tiles[r + per_sft // 2], tiles[r]) for r in range(per_sft // 2)]
+    return [tile[0:1] for tile in block_transposes(tiles)]
+
+
+def late_row():
+    return NB // LANES
+
+
+def early_row():
+    return 2 * (NB // LANES) * (SFT_DEV + 1)
+
+
+def series_kernel(band_ref, mine_ref, far_ref, twist_ref, table_ref, time_ref, z_ref):
+    band = band_ref[0]
+    first = band == 0
+    half = NP // 2
+    per_sft = NB // LANES
+    own = [[None, None] for _ in range(NP)]
+    inner = [[None, None] for _ in range(NP)]
+    for part in range(2):
+        for kappa in range(half):
+            cols = pl.ds(LANES * kappa, LANES)
+            rows = pl.ds(pl.multiple_of(band * SFT_DEV, SFT_DEV), SFT_DEV)
+            mine, far = mine_ref[part, rows, cols], far_ref[part, rows, cols]
+            own[kappa][part] = jnp.where(first, mine, far)
+            own[kappa + half][part] = jnp.where(first, far, mine)
+            mine, far = [
+                jnp.where(first, ref[part, pl.ds(SFT_DEV, 1), cols], ref[part, pl.ds(SFT_DEV - 1, 1), cols])
+                for ref in (mine_ref, far_ref)
+            ]
+            inner[kappa][part] = jnp.where(first, mine, far)
+            inner[kappa + half][part] = jnp.where(first, far, mine)
+    inverse_columns([tuple(v) for v in own], twist_ref, z_ref, [pl.ds(p, ROWS, stride=NP) for p in range(NP)])
+    inverse_columns([tuple(v) for v in inner], twist_ref, z_ref, [pl.ds(LANES + p, 1) for p in range(NP)])
+    z_ref[:, pl.ds(LANES + NP, LANES - NP), :] = jnp.zeros((2, LANES - NP, LANES), jnp.float32)
+    grid = inverse_grid(table_ref, z_ref)
+    inner_row = jnp.where(first, early_row(), late_row())
+    for part in range(2):
+        tiles = [grid[NQ * part + ROWS * r : NQ * part + ROWS * (r + 1), :LANES] for r in range(per_sft)]
+        tiles = block_transposes(tiles)
+        for r in range(per_sft):
+            time_ref[pl.ds(2 * (per_sft + r) + part, ROWS, stride=2 * per_sft), :] = tiles[r]
+        tiles = halo_rows(grid[:, LANES:], part, jnp.logical_not(first))
+        for r in range(per_sft // 2):
+            time_ref[pl.ds(inner_row + 2 * r + part, 1), :] = tiles[r]
+
+
 def resample_kernel(
     band_ref,
     start_in_ref,
-    local_ref,
-    far_ref,
-    same_ref,
-    other_ref,
+    series_ref,
+    outer_ref,
     fraction_ref,
     weights_ref,
     sums_ref,
@@ -351,7 +428,6 @@
     table_ref,
     out_ref,
     z_ref,
-    grid_ref,
     time_ref,
     run_ref,
     start_ref,
@@ -359,57 +435,21 @@
 ):
     starts_copy = pltpu.make_async_copy(start_in_ref, start_ref, copy_sem)
     starts_copy.start()
-    band = band_ref[0]
-    first = band == 0
-    half = NP // 2
+    first = band_ref[0] == 0
     owners = out_ref.shape[0]
     slot = out_ref.shape[1]
     tmpl_local = start_ref.shape[0] // SFT_DEV
-    row = lax.broadcasted_iota(jnp.int32, (ROWS, LANES), 0)
     lane = lax.broadcasted_iota(jnp.int32, (ROWS, LANES), 1)
-    for group in range(2):
-        values = [[None, None] for _ in range(NP)]
-        for part in range(2):
-            for kappa in range(half):
-                cols = pl.ds(LANES * kappa, LANES)
-                if group == 0:
-                    rows = pl.ds(pl.multiple_of(band * SFT_DEV, SFT_DEV), SFT_DEV)
-                    mine = local_ref[part, rows, cols]
-                    far = far_ref[part, rows, cols]
-                else:
-                    inner = [
-                        jnp.where(first, ref[part, pl.ds(SFT_DEV, 1), cols], ref[part, pl.ds(SFT_DEV - 1, 1), cols])
-                        for ref in (local_ref, far_ref)
-                    ]
-                    mine = jnp.where(row == 0, same_ref[part, :, cols], inner[0])
-                    far = jnp.where(row == 0, other_ref[part, :, cols], inner[1])
-                values[kappa][part] = jnp.where(first, mine, far)
-                values[kappa + half][part] = jnp.where(first, far, mine)
-        values = small_fft([tuple(value) for value in values], 1.0)
-        for p in range(NP):
-            turned = times(values[p], twist_ref[0, pl.ds(p, 1), :], twist_ref[1, pl.ds(p, 1), :])
-            for part in range(2):
-                z_ref[part, pl.ds(LANES * group + p, ROWS, stride=NP), :] = turned[part]
-    dims = (((1,), (1,)), ((), ()))
-    z_value = split_value(jnp.concatenate([z_ref[0], z_ref[1]], axis=1))
-    grid_ref[...] = split_dot((table_ref[0], table_ref[1]), z_value, dims)
-    per_sft = NB // LANES
-    late_row = 2 * (per_sft // 2)
-    early_row = 2 * per_sft * (SFT_DEV + 1)
-    outer_row = jnp.where(first, late_row, early_row)
-    inner_row = jnp.where(first, early_row, late_row)
-    take_late = (lane < NP) == first
+    values = [tuple(outer_ref[part, pl.ds(kappa, 1), :] for part in range(2)) for kappa in range(NP)]
+    z_ref[:, pl.ds(NP, LANES - NP), :] = jnp.zeros((2, LANES - NP, LANES), jnp.float32)
+    inverse_columns(values, twist_ref, z_ref, [pl.ds(p, 1) for p in range(NP)])
+    grid = inverse_grid(table_ref, z_ref)
+    time_ref[...] = series_ref[...]
+    outer_row = jnp.where(first, late_row(), early_row())
     for part in range(2):
-        tiles = [grid_ref[pl.ds(NQ * part + ROWS * r, ROWS), pl.ds(0, LANES)] for r in range(per_sft)]
-        tiles = block_transposes(tiles)
-        for r in range(per_sft):
-            time_ref[pl.ds(2 * (per_sft + r) + part, ROWS, stride=2 * per_sft), :] = tiles[r]
-        tiles = [grid_ref[pl.ds(NQ * part + ROWS * r, ROWS), pl.ds(LANES, LANES)] for r in range(per_sft)]
-        tiles = [jnp.where(take_late, tiles[r + per_sft // 2], tiles[r]) for r in range(per_sft // 2)]
-        tiles = block_transposes(tiles)
-        for r in range(per_sft // 2):
-            time_ref[pl.ds(outer_row + 2 * r + part, 1), :] = tiles[r][0:1]
-            time_ref[pl.ds(inner_row + 2 * r + part, 1), :] = tiles[r][1:2]
+        tiles = halo_rows(grid, part, first)
+        for r in range(NB // LANES // 2):
+            time_ref[pl.ds(outer_row + 2 * r + part, 1), :] = tiles[r]
     for j in range(owners):
         out_ref[j, pl.ds(slot - ROWS, ROWS), :] = sums_ref[...]
     starts_copy.wait()
@@ -535,26 +575,6 @@
     return pltpu.with_memory_space_constraint(value, pltpu.VMEM)
 
 
-def exchange_bins(sft_bins):
-    owner_count = lax.axis_size("tm") * lax.axis_size("band")
-    first = lax.axis_index("band") == 0
-    axes = ("tm", "band")
-    straight, crossed = [], []
-    for rank in range(owner_count):
-        up = rank % 2 == 0
-        target = rank + 2 if up else rank - 2
-        if 0 <= target < owner_count:
-            straight.append((rank, target))
-        target = rank - 1 if up else rank + 1
-        if 0 <= target < owner_count:
-            crossed.append((rank, target))
-    far = lax.ppermute(sft_bins, "band", [(0, 1), (1, 0)])
-    tail, head = sft_bins[:, -1:], sft_bins[:, :1]
-    same = lax.ppermute(jnp.where(first, tail, head), axes, straight)
-    other = lax.ppermute(jnp.where(first, head, tail), axes, crossed)
-    return far, same, other
-
-
 def run_device(sft_bins, delay_code, antenna):
     axes = ("tm", "band")
     owners = lax.axis_size("tm") * lax.axis_size("band")
@@ -563,37 +583,59 @@
     tmpl_local = delay_code.shape[0]
     f32 = jnp.float32
     slot = SFT_DEV * ROWS
-    far, same, other = exchange_bins(sft_bins)
-    fraction, weights, sums, starts = pl.pallas_call(
+    time_rows = 2 * (SFT_DEV + 2) * NB // LANES
+    smem = pl.BlockSpec(memory_space=pltpu.SMEM)
+    band = lax.axis_index("band").astype(jnp.int32).reshape(1)
+    far = lax.ppermute(sft_bins, "band", [(0, 1), (1, 0)])
+    fraction, weights, sums, starts, mine = pl.pallas_call(
         prepare_kernel,
         out_shape=(
             pltpu.VMEM((tmpl_local * SFT_DEV * 2 * ROWS, LANES), f32),
             pltpu.VMEM((tmpl_local * 2 * SFT_DEV * 2 * ROWS, LANES), f32),
             pltpu.VMEM((ROWS, LANES), f32),
             pltpu.VMEM((tmpl_local * SFT_DEV, LANES), jnp.int32),
+            pltpu.VMEM(sft_bins.shape, f32),
         ),
-        in_specs=[vmem(), vmem()],
-        out_specs=(vmem(),) * 4,
+        in_specs=[vmem()] * 3,
+        out_specs=(vmem(),) * 5,
         name="prepare",
-    )(resident(delay_code), resident(antenna))
-    twist, inverse_table = inverse_tables()
-    band = lax.axis_index("band").astype(jnp.int32).reshape(1)
-    operands = [starts, sft_bins, far, same, other, fraction, weights, sums, jnp.asarray(twist), jnp.asarray(inverse_table)]
+    )(delay_code, antenna, sft_bins)
+    far, mine = resident(far), resident(mine)
+    edge = pl.pallas_call(
+        pack_kernel,
+        out_shape=pltpu.VMEM((2, NP, LANES), f32),
+        in_specs=[smem, vmem(), vmem()],
+        out_specs=vmem(),
+        name="pack",
+    )(band, mine, far)
+    along = [(rank, rank + 2) for rank in range(0, owners - 2, 2)]
+    along += [(rank, rank - 2) for rank in range(3, owners, 2)]
+    outer = lax.ppermute(edge, axes, along)
+    twist, inverse_table = [resident(jnp.asarray(table)) for table in inverse_tables()]
+    series = pl.pallas_call(
+        series_kernel,
+        out_shape=pltpu.VMEM((time_rows, LANES), f32),
+        in_specs=[smem] + [vmem()] * 4,
+        out_specs=vmem(),
+        scratch_shapes=[pltpu.VMEM((2, 2 * LANES, LANES), f32)],
+        name="series",
+    )(band, mine, far, twist, inverse_table)
+    operands = [resident(value) for value in (starts, series, outer, fraction, weights, sums)]
+    operands += [twist, inverse_table]
     samples = pl.pallas_call(
         resample_kernel,
         out_shape=pltpu.VMEM((owners, 2 * slot + ROWS, LANES), f32),
-        in_specs=[pl.BlockSpec(memory_space=pltpu.SMEM)] + [vmem()] * len(operands),
+        in_specs=[smem] + [vmem()] * len(operands),
         out_specs=vmem(),
         scratch_shapes=[
-            pltpu.VMEM((2, 2 * LANES, LANES), f32),
-            pltpu.VMEM((2 * LANES, 2 * LANES), f32),
-            pltpu.VMEM((2 * (SFT_DEV + 2) * NB // LANES, LANES), f32),
+            pltpu.VMEM((2, LANES, LANES), f32),
+            pltpu.VMEM((time_rows, LANES), f32),
             pltpu.VMEM((tmpl_local * owners * ROWS, LANES), f32),
             pltpu.SMEM((tmpl_local * SFT_DEV, LANES), jnp.int32),
             pltpu.SemaphoreType.DMA,
         ],
         name="resample",
-    )(band, *[resident(operand) for operand in operands])
+    )(band, *operands)
     samples = lax.all_to_all(samples, axes, split_axis=0, concat_axis=0, tiled=True)
     parts, totals = pl.pallas_call(
         section_kernel,

time: 54.3 us -> 52.7 us (0.971)
  waiting for transfers between devices: 12.7 us -> 15.2 us
  blocking collectives: 21.5 us -> 19.3 us
  local copies, waits for them, and re-layouts: 2.15 us -> 0.02 us
  Pallas kernels: 5.25 us -> 6.84 us
  other arithmetic: 1.61 us -> 0.69 us
    ppermute x3 -> x2, waiting for transfers between devices: 0.01 us -> 2.87 us  [the longest x1 2.06 us: run_device(): far = lax.ppermute(sft_bins, 'band', [(0, 1), (1, 0)])]
    all_to_all x1, blocking collectives: 21.5 us -> 19.3 us  [run_device(): lax.all_to_all(samples, axes, split_axis=0, concat_axis=0, tiled=True)]
    unnamed x12 -> x6, local copies, waits for them, and re-layouts: 2.15 us -> 0.02 us
    pallas_call x1, Pallas kernels: 0.64 us -> 1.62 us  [run_device(): pl.pallas_call(prepare_kernel, out_shape=(pltpu.VMEM((tmpl_local * SFT_DE...]
    select_n x1 -> x0, other arithmetic: 0.92 us -> none  [exchange_bins(): other = lax.ppermute(jnp.where(first, head, tail), axes, crossed)]
    pallas_call x0 -> x2, Pallas kernels: none -> 0.61 us  [the longest x1 0.59 us: run_device(): pl.pallas_call(series_kernel, out_shape=pltpu.VMEM((time_rows, LANES), f3...]
    ppermute x3 -> x2, starting transfers between devices: 7.11 us -> 6.7 us  [the longest x1 3.73 us: run_device(): outer = lax.ppermute(edge, axes, along)]
  transfers between devices with their start and end apart: 4 -> 3, of which waited for: 1 -> 3; matrix products, arithmetic and copies ran while one was open for 3% -> 1% of each run, Pallas kernels for 1% -> 4%
where the time goes in v3:
time: 52.7 us; the launch traced here: 52.4 us
  blocking collectives  19.3 us (37%)
  waiting for transfers between devices  15.2 us (29%)
  starting transfers between devices  10.2 us (19%)
  Pallas kernels  6.84 us (13%)
  other arithmetic  0.69 us (1%)
    all_to_all x1, blocking collectives, run_device(): lax.all_to_all(samples, axes, split_axis=0, concat_axis=0, tiled=True)  19.3 us
    all_to_all x1, waiting for transfers between devices, run_device(): parts = lax.all_to_all(parts, axes, split_axis=0, concat_axis=0, tiled=True)  12.3 us
    ppermute x1, starting transfers between devices, run_device(): outer = lax.ppermute(edge, axes, along)  3.73 us
    all_to_all x1, starting transfers between devices, run_device(): parts = lax.all_to_all(parts, axes, split_axis=0, concat_axis=0, tiled=True)  3.49 us
    ppermute x1, starting transfers between devices, run_device(): far = lax.ppermute(sft_bins, 'band', [(0, 1), (1, 0)])  2.97 us
    pallas_call x1, Pallas kernels, run_device(): pl.pallas_call(resample_kernel, out_shape=pltpu.VMEM((owners, 2 * slot +...  2.33 us
    ppermute x1, waiting for transfers between devices, run_device(): far = lax.ppermute(sft_bins, 'band', [(0, 1), (1, 0)])  2.06 us
    pallas_call x1, Pallas kernels, run_device(): pl.pallas_call(prepare_kernel, out_shape=(pltpu.VMEM((tmpl_local * SFT_DE...  1.62 us
  transfers between devices with their start and end apart: 3, of which 3 were waited for; matrix products, arithmetic and copies ran while one was open for 1% of the time, Pallas kernels for 4%

profile of v3, /device:TPU:0, one launch (start us, length us, event | category | flops | bytes accessed | tf_op | source)
XLA Modules:
  0.0 52.4 jit_solution(4734312923874013962)
XLA Ops:
  0.0 3.0 %collective-permute-start = (f32[2,16,1024]{2,1,0:T(8,128)}, f32[2,16,1024]{2,1,0:T(8,128)S(1)}, u32[]{:S(2)}, u32[]{:S(2)}) collective-permute-start(f32[2,16,1024]{2,1,0:T(8,128)} %bins_ref.1), channel_id=1, source_target_pairs={{0,2},{2,0},{1,3},{3,1},{4,6},{6,4},{5,7},{7,5},{8,10},{10,8},{9,1... | collective-permute-start | bytes 393224 | tf_op jit(solution)/shard_map/ppermute | solution.py:589
  3.0 1.6 %prepare.1 = (f32[256,128]{1,0:T(8,128)S(1)}, f32[512,128]{1,0:T(8,128)S(1)}, f32[8,128]{1,0:T(8,128)S(1)}, s32[16,128]{1,0:T(8,128)S(1)}, f32[2,16,1024]{2,1,0:T(8,128)S(1)}) custom-call(s32[2,128,128]{2,1,0:T(8,128)} %code_ref.1, f32[2,2,128,128]{3,2,1,0:T(8,128)} %antenna_ref.1, f32[2,16,1024]{2,1,0:T(8,128)} %bins_ref.1), custom_call_target="tpu_custom_call" | custom-call | tf_op jit(solution)/shard_map/prepare/pallas_call | solution.py:590
  4.6 0.0 copy-start
  4.6 2.1 %collective-permute-done.far_ref = f32[2,16,1024]{2,1,0:T(8,128)S(1)} collective-permute-done((f32[2,16,1024]{2,1,0:T(8,128)}, f32[2,16,1024]{2,1,0:T(8,128)S(1)}, u32[]{:S(2)}, u32[]{:S(2)}) %collective-permute-start) | collective-permute-done | bytes 131104 | tf_op jit(solution)/shard_map/ppermute | solution.py:589
  6.7 0.0 copy-start.2
  6.7 3.7 %collective-permute-start.1 = (f32[2,16,128]{2,1,0:T(8,128)S(1)}, f32[2,16,128]{2,1,0:T(8,128)S(1)}, u32[]{:S(2)}, u32[]{:S(2)}) collective-permute-start(f32[2,16,128]{2,1,0:T(8,128)S(1)} %pack.1), channel_id=1, source_target_pairs={{0,4},{4,8},{8,12},{6,2},{10,6},{14,10},{1,5},{5,9},{9,13},{7,3},{... | collective-permute-start | bytes 49160 | tf_op jit(solution)/shard_map/ppermute | solution.py:613
  10.4 0.0 copy-done
  10.4 0.0 copy-done.2
  10.5 0.6 %series.1.series_ref = f32[320,128]{1,0:T(8,128)S(1)} custom-call(s32[1]{0:T(128)} %bitcast.band_ref, f32[2,16,1024]{2,1,0:T(8,128)S(1)} %get-tuple-element.13.mine_ref, f32[2,16,1024]{2,1,0:T(8,128)S(1)} %collective-permute-done.far_ref, f32[2,16,128]{2,1,0:T(8,128)S(1)} %copy-done.2, bf16[2,256,256]{2,1,0:T(8,128)(2,1)S(1)} %copy-done), custom_call_target="tpu_custom_call" | custom-call | tf_op jit(solution)/shard_map/series/pallas_call | solution.py:615
  11.1 0.8 %collective-permute-done.1.outer_ref = f32[2,16,128]{2,1,0:T(8,128)S(1)} collective-permute-done((f32[2,16,128]{2,1,0:T(8,128)S(1)}, f32[2,16,128]{2,1,0:T(8,128)S(1)}, u32[]{:S(2)}, u32[]{:S(2)}) %collective-permute-start.1) | collective-permute-done | bytes 16416 | tf_op jit(solution)/shard_map/ppermute | solution.py:613
  11.9 2.3 %resample.1 = f32[8,136,128]{2,1,0:T(8,128)S(1)} custom-call(s32[1]{0:T(128)} %bitcast.band_ref, s32[16,128]{1,0:T(8,128)S(1)} %get-tuple-element.12.start_in_ref, f32[320,128]{1,0:T(8,128)S(1)} %series.1.series_ref, f32[2,16,128]{2,1,0:T(8,128)S(1)} %collective-permute-done.1.outer_ref, f32[256,128]{1,0:T(8,128)S(1)} %get-tuple-element.14.fraction_ref, ...), custom_call_target="tpu_custom_call" | custom-call | tf_op jit(solution)/shard_map/resample/pallas_call | solution.py:625
  14.2 19.3 %all_to_all.10.samples_ref = f32[8,136,128]{2,1,0:T(8,128)S(1)} all-to-all(f32[8,136,128]{2,1,0:T(8,128)S(1)} %resample.1), channel_id=1, replica_groups=mesh['groups'=2,'tm'=4,'band'=2,'tmpl'=2] {'tm','band'}, dimensions={0} | all-to-all | bytes 1114112 | tf_op jit(solution)/shard_map/all_to_all | solution.py:639
  33.5 1.0 %section.1 = (f32[8,128,128]{2,1,0:T(8,128)}, f32[8,128]{1,0:T(8,128)S(1)}) custom-call(f32[8,136,128]{2,1,0:T(8,128)S(1)} %all_to_all.10.samples_ref), custom_call_target="tpu_custom_call" | custom-call | tf_op jit(solution)/shard_map/section/pallas_call | solution.py:640
  34.5 3.5 %all-to-all-start.1 = ((f32[8,128,128]{2,1,0:T(8,128)}), f32[8,128,128]{2,1,0:T(8,128)S(1)}, u32[]{:S(2)}, u32[]{:S(2)}) async-start(f32[8,128,128]{2,1,0:T(8,128)} %get-tuple-element.17), calls=%async_computation.1 | async-start | bytes 1048576 | tf_op jit(solution)/shard_map/all_to_all | solution.py:648
  38.1 0.6 %fusion.9 = (f32[1,128,128]{2,1,0:T(8,128)S(1)}, f32[1,128,128]{2,1,0:T(8,128)S(1)}, f32[1,128,128]{2,1,0:T(8,128)S(1)}, f32[1,128,128]{2,1,0:T(8,128)S(1)}) fusion(s32[128]{0:T(128)S(1)} %iota_shift-right-logical_fusion, s32[128]{0:T(128)S(1)} %broadcast_add_fusion.1, pred[128]{0:T(512)(128)(4,1)S(1)} %compare_and_fusion.1, s32[128]{0:T(128)S(1)} %iota_and_fusion, ...), kind=kLoop, calls=%fused_computation.20 | loop fusion | flops 557056 | bytes 264452 | tf_op jit(solution)/shard_map/cos | solution.py:42
  38.8 0.0 copy-start.1
  38.8 12.3 %all-to-all-done.1.parts_ref = f32[8,128,128]{2,1,0:T(8,128)S(1)} async-done(((f32[8,128,128]{2,1,0:T(8,128)}), f32[8,128,128]{2,1,0:T(8,128)S(1)}, u32[]{:S(2)}, u32[]{:S(2)}) %all-to-all-start.1) | async-done | bytes 524320 | tf_op jit(solution)/shard_map/all_to_all | solution.py:648
  51.1 0.0 copy-done.1
  51.1 1.3 %statistic.1 = f32[2,128,128]{2,1,0:T(8,128)} custom-call(f32[8,128,128]{2,1,0:T(8,128)S(1)} %all-to-all-done.1.parts_ref, f32[8,128]{1,0:T(8,128)S(1)} %get-tuple-element.18.sums_ref, f32[2,128,128]{2,1,0:T(8,128)S(1)} %get-tuple-element.23.coarse_ref, f32[2,128,128]{2,1,0:T(8,128)S(1)} %get-tuple-element.24.fine_ref, bf16[2,256,256]{2,1,0:T(8,128)(2,1)S(1)} %copy-done.1), custom_call_target="tpu_custom_call" | custom-call | tf_op jit(solution)/shard_map/statistic/pallas_call | solution.py:656
  (8 shorter events, 0.1 us)
Async XLA Ops:
  0.0 6.7 %collective-permute-start = (f32[2,16,1024]{2,1,0:T(8,128)}, f32[2,16,1024]{2,1,0:T(8,128)S(1)}, u32[]{:S(2)}, u32[]{:S(2)}) collective-permute-start(f32[2,16,1024]{2,1,0:T(8,128)} %bins_ref.1), channel_id=1, source_target_pairs={{0,2},{2,0},{1,3},{3,1},{4,6},{6,4},{5,7},{7,5},{8,10},{10,8},{9,1... | collective-permute-start | bytes 393224 | tf_op jit(solution)/shard_map/ppermute | solution.py:589
  4.6 5.8 %copy-start = (bf16[2,256,256]{2,1,0:T(8,128)(2,1)S(1)}, bf16[2,256,256]{2,1,0:T(8,128)(2,1)}, u32[]{:S(2)}) copy-start(bf16[2,256,256]{2,1,0:T(8,128)(2,1)} %constant.84.clone.table_ref) | copy-start | bytes 786436
  6.7 3.8 %copy-start.2 = (f32[2,16,128]{2,1,0:T(8,128)S(1)}, f32[2,16,128]{2,1,0:T(8,128)}, u32[]{:S(2)}) copy-start(f32[2,16,128]{2,1,0:T(8,128)} %constant.83.clone.twist_ref) | copy-start | bytes 49156
  6.7 5.2 %collective-permute-start.1 = (f32[2,16,128]{2,1,0:T(8,128)S(1)}, f32[2,16,128]{2,1,0:T(8,128)S(1)}, u32[]{:S(2)}, u32[]{:S(2)}) collective-permute-start(f32[2,16,128]{2,1,0:T(8,128)S(1)} %pack.1), channel_id=1, source_target_pairs={{0,4},{4,8},{8,12},{6,2},{10,6},{14,10},{1,5},{5,9},{9,13},{7,3},{... | collective-permute-start | bytes 49160 | tf_op jit(solution)/shard_map/ppermute | solution.py:613
  34.5 16.6 %all-to-all-start.1 = ((f32[8,128,128]{2,1,0:T(8,128)}), f32[8,128,128]{2,1,0:T(8,128)S(1)}, u32[]{:S(2)}, u32[]{:S(2)}) async-start(f32[8,128,128]{2,1,0:T(8,128)} %get-tuple-element.17), calls=%async_computation.1 | async-start | bytes 1048576 | tf_op jit(solution)/shard_map/all_to_all | solution.py:648
  38.8 12.4 %copy-start.1 = (bf16[2,256,256]{2,1,0:T(8,128)(2,1)S(1)}, bf16[2,256,256]{2,1,0:T(8,128)(2,1)}, u32[]{:S(2)}) copy-start(bf16[2,256,256]{2,1,0:T(8,128)(2,1)} %constant.85.clone.table_ref) | copy-start | bytes 786436

commit v4 on v3

--- a/solution.py
+++ b/solution.py
@@ -302,7 +302,7 @@
     return high, (value - high.astype(jnp.float32)).astype(jnp.bfloat16)
 
 
-def prepare_kernel(code_ref, antenna_ref, bins_ref, fraction_ref, weights_ref, sums_ref, start_ref, mine_ref):
+def prepare_kernel(code_ref, antenna_ref, bins_ref, fraction_ref, weights_ref, sums_ref, start_ref, shift_ref, mine_ref):
     mine_ref[...] = bins_ref[...]
     tmpl_local = code_ref.shape[0]
     owners = code_ref.shape[1] // (2 * ROWS)
@@ -315,8 +315,10 @@
             if h == 0:
                 starts = jnp.zeros((ROWS, LANES), jnp.int32)
                 for j in range(owners):
-                    starts = jnp.where(lane == j, jnp.broadcast_to(turned[j][:, 0:1], (ROWS, LANES)), starts)
-                starts = starts // NFRAC - MAXD + (row * owners + lane) * RUN + (NB - 1)
+                    whole = jnp.broadcast_to(turned[j][:, 0:1], (ROWS, LANES)) // NFRAC - MAXD
+                    start = whole + (row * owners + j) * RUN + (NB - 1)
+                    starts = jnp.where(lane == j, start, starts)
+                    shift_ref[pl.ds(t * SFT_DEV * owners + j, ROWS, stride=owners), :] = start & (LANES - 1)
                 start_ref[pl.ds(t * ROWS, ROWS), :] = starts
             for j in range(owners):
                 level = (turned[j] & (NFRAC - 1)).astype(jnp.float32) * (1.0 / NFRAC)
@@ -381,7 +383,70 @@
     return 2 * (NB // LANES) * (SFT_DEV + 1)
 
 
-def series_kernel(band_ref, mine_ref, far_ref, twist_ref, table_ref, time_ref, z_ref):
+def align_runs(time_ref, start_ref, run_ref, s_local, place):
+    tmpl_local = start_ref.shape[0] // SFT_DEV
+    owners = NB // RUN
+    starts = [start_ref[t * SFT_DEV + s_local, j] for t in range(tmpl_local) for j in range(owners)]
+    tiles = [time_ref[pl.ds((start >> 7) * 2, ROWS), :] for start in starts]
+    tiles = [pltpu.roll(tile, (-start) & (LANES - 1), 1) for tile, start in zip(tiles, starts)]
+    for at, tile in enumerate(tiles):
+        run_ref[pl.ds((place * len(tiles) + at) * ROWS, ROWS), :] = tile
+
+
+def combine_runs(run_ref, shift_ref, fraction_ref, weights_ref, flat_ref, slot, s_local, place):
+    tmpl_local = shift_ref.shape[0] // (SFT_DEV * ROWS)
+    owners = NB // RUN
+    lane = lax.broadcasted_iota(jnp.int32, (ROWS, LANES), 1)
+
+    def rows_at(group):
+        return pl.ds(group * ROWS if isinstance(group, int) else pl.multiple_of(group * ROWS, ROWS), ROWS)
+
+    for t in range(tmpl_local):
+        straight = lane < LANES - shift_ref[rows_at(t * SFT_DEV + s_local), :]
+        rows = []
+        for part in range(2):
+            base = (place * tmpl_local + t) * owners * ROWS + part
+            raw = [run_ref[pl.ds(base + 2 * i, ROWS, stride=ROWS), :] for i in range(4)]
+            rows.append([jnp.where(straight, raw[i], raw[i + 1]) for i in range(3)])
+        at = (t * SFT_DEV + s_local) * 2
+        coeffs = [lagrange(fraction_ref[rows_at(at + h), :]) for h in range(2)]
+        totals = [[coeffs[h][0] * rows[part][h] for h in range(2)] for part in range(2)]
+        for k in range(1, 4):
+            rolled = [[pltpu.roll(tile, LANES - k, 1) for tile in rows[part]] for part in range(2)]
+            for part in range(2):
+                for h in range(2):
+                    tap = jnp.where(lane < LANES - k, rolled[part][h], rolled[part][h + 1])
+                    totals[part][h] = totals[part][h] + coeffs[h][k] * tap
+        for w in range(2):
+            at = ((t * 2 + w) * SFT_DEV + s_local) * 2
+            for h in range(2):
+                weight = weights_ref[rows_at(at + h), :]
+                for part in range(2):
+                    to = (part * SFT_DEV + s_local) * ROWS + t * 4 + w * 2 + h
+                    flat_ref[pl.ds(to, owners, stride=slot), :] = totals[part][h] * weight
+
+
+def series_kernel(
+    band_ref,
+    mine_ref,
+    far_ref,
+    twist_ref,
+    table_ref,
+    start_in_ref,
+    shift_ref,
+    fraction_ref,
+    weights_ref,
+    sums_ref,
+    time_ref,
+    out_ref,
+    z_ref,
+    run_ref,
+    start_ref,
+    copy_sem,
+):
+    starts_copy = pltpu.make_async_copy(start_in_ref, start_ref, copy_sem)
+    starts_copy.start()
+    owners, slot = out_ref.shape[:2]
     band = band_ref[0]
     first = band == 0
     half = NP // 2
@@ -416,16 +481,28 @@
             time_ref[pl.ds(inner_row + 2 * r + part, 1), :] = tiles[r]
 
 
+    for j in range(owners):
+        out_ref[j, pl.ds(slot - ROWS, ROWS), :] = sums_ref[...]
+    starts_copy.wait()
+    flat_ref = out_ref.reshape(owners * slot, LANES)
+    order = list(range(1, SFT_DEV - 1)) + [jnp.where(first, SFT_DEV - 1, 0)]
+    for place, s_local in enumerate(order):
+        align_runs(time_ref, start_ref, run_ref, s_local, place)
+    for place, s_local in enumerate(order):
+        combine_runs(run_ref, shift_ref, fraction_ref, weights_ref, flat_ref, slot, s_local, place)
+
+
 def resample_kernel(
     band_ref,
     start_in_ref,
     series_ref,
     outer_ref,
+    shift_ref,
     fraction_ref,
     weights_ref,
-    sums_ref,
     twist_ref,
     table_ref,
+    partial_ref,
     out_ref,
     z_ref,
     time_ref,
@@ -436,10 +513,7 @@
     starts_copy = pltpu.make_async_copy(start_in_ref, start_ref, copy_sem)
     starts_copy.start()
     first = band_ref[0] == 0
-    owners = out_ref.shape[0]
-    slot = out_ref.shape[1]
-    tmpl_local = start_ref.shape[0] // SFT_DEV
-    lane = lax.broadcasted_iota(jnp.int32, (ROWS, LANES), 1)
+    owners, slot = out_ref.shape[:2]
     values = [tuple(outer_ref[part, pl.ds(kappa, 1), :] for part in range(2)) for kappa in range(NP)]
     z_ref[:, pl.ds(NP, LANES - NP), :] = jnp.zeros((2, LANES - NP, LANES), jnp.float32)
     inverse_columns(values, twist_ref, z_ref, [pl.ds(p, 1) for p in range(NP)])
@@ -450,53 +524,11 @@
         tiles = halo_rows(grid, part, first)
         for r in range(NB // LANES // 2):
             time_ref[pl.ds(outer_row + 2 * r + part, 1), :] = tiles[r]
-    for j in range(owners):
-        out_ref[j, pl.ds(slot - ROWS, ROWS), :] = sums_ref[...]
     starts_copy.wait()
     flat_ref = out_ref.reshape(owners * slot, LANES)
-
-    def one_sft(s_local, carry):
-        for t in range(tmpl_local):
-            starts = [start_ref[t * SFT_DEV + s_local, j] for j in range(owners)]
-            shifts = [start & (LANES - 1) for start in starts]
-            tiles = [time_ref[pl.ds((start >> 7) * 2, ROWS), :] for start in starts]
-            tiles = [pltpu.roll(tile, (LANES - shift) & (LANES - 1), 1) for tile, shift in zip(tiles, shifts)]
-            later = [pltpu.roll(tile, ROWS - 2, 0) for tile in tiles]
-            for j in range(owners):
-                run_ref[pl.ds((t * owners + j) * ROWS, ROWS), :] = jnp.where(
-                    lane < LANES - shifts[j], tiles[j], later[j]
-                )
-        rows = [
-            [
-                [run_ref[pl.ds(t * owners * ROWS + 2 * i + part, ROWS, stride=ROWS), :] for i in range(3)]
-                for part in range(2)
-            ]
-            for t in range(tmpl_local)
-        ]
-        for t in range(tmpl_local):
-            at = (t * SFT_DEV + s_local) * 2
-            coeffs = [lagrange(fraction_ref[pl.ds((at + h) * ROWS, ROWS), :]) for h in range(2)]
-            weights = [
-                [
-                    weights_ref[pl.ds((((t * 2 + w) * SFT_DEV + s_local) * 2 + h) * ROWS, ROWS), :]
-                    for h in range(2)
-                ]
-                for w in range(2)
-            ]
-            for part in range(2):
-                totals = [coeffs[h][0] * rows[t][part][h] for h in range(2)]
-                for k in range(1, 4):
-                    rolled = [pltpu.roll(tile, LANES - k, 1) for tile in rows[t][part]]
-                    for h in range(2):
-                        tap = jnp.where(lane < LANES - k, rolled[h], rolled[h + 1])
-                        totals[h] = totals[h] + coeffs[h][k] * tap
-                for w in range(2):
-                    for h in range(2):
-                        at = (part * SFT_DEV + s_local) * ROWS + t * 4 + w * 2 + h
-                        flat_ref[pl.ds(at, owners, stride=slot), :] = totals[h] * weights[w][h]
-        return carry
-
-    lax.fori_loop(0, SFT_DEV, one_sft, 0)
+    s_local = jnp.where(first, 0, SFT_DEV - 1)
+    align_runs(time_ref, start_ref, run_ref, s_local, 0)
+    combine_runs(run_ref, shift_ref, fraction_ref, weights_ref, flat_ref, slot, s_local, 0)
 
 
 def section_kernel(samples_ref, out_ref, sums_ref, mid_ref):
@@ -587,17 +619,18 @@
     smem = pl.BlockSpec(memory_space=pltpu.SMEM)
     band = lax.axis_index("band").astype(jnp.int32).reshape(1)
     far = lax.ppermute(sft_bins, "band", [(0, 1), (1, 0)])
-    fraction, weights, sums, starts, mine = pl.pallas_call(
+    fraction, weights, sums, starts, shifts, mine = pl.pallas_call(
         prepare_kernel,
         out_shape=(
             pltpu.VMEM((tmpl_local * SFT_DEV * 2 * ROWS, LANES), f32),
             pltpu.VMEM((tmpl_local * 2 * SFT_DEV * 2 * ROWS, LANES), f32),
             pltpu.VMEM((ROWS, LANES), f32),
             pltpu.VMEM((tmpl_local * SFT_DEV, LANES), jnp.int32),
+            pltpu.VMEM((tmpl_local * SFT_DEV * owners, LANES), jnp.int32),
             pltpu.VMEM(sft_bins.shape, f32),
         ),
         in_specs=[vmem()] * 3,
-        out_specs=(vmem(),) * 5,
+        out_specs=(vmem(),) * 6,
         name="prepare",
     )(delay_code, antenna, sft_bins)
     far, mine = resident(far), resident(mine)
@@ -612,28 +645,40 @@
     along += [(rank, rank - 2) for rank in range(3, owners, 2)]
     outer = lax.ppermute(edge, axes, along)
     twist, inverse_table = [resident(jnp.asarray(table)) for table in inverse_tables()]
-    series = pl.pallas_call(
+    fraction, weights, sums, starts, shifts = [
+        resident(value) for value in (fraction, weights, sums, starts, shifts)
+    ]
+    payload = pltpu.VMEM((owners, 2 * slot + ROWS, LANES), f32)
+    scratch = [
+        pltpu.SMEM((tmpl_local * SFT_DEV, LANES), jnp.int32),
+        pltpu.SemaphoreType.DMA,
+    ]
+    series, partial = pl.pallas_call(
         series_kernel,
-        out_shape=pltpu.VMEM((time_rows, LANES), f32),
-        in_specs=[smem] + [vmem()] * 4,
-        out_specs=vmem(),
-        scratch_shapes=[pltpu.VMEM((2, 2 * LANES, LANES), f32)],
+        out_shape=(pltpu.VMEM((time_rows, LANES), f32), payload),
+        in_specs=[smem] + [vmem()] * 9,
+        out_specs=(vmem(), vmem()),
+        scratch_shapes=[
+            pltpu.VMEM((2, 2 * LANES, LANES), f32),
+            pltpu.VMEM(((SFT_DEV - 1) * tmpl_local * owners * ROWS, LANES), f32),
+        ]
+        + scratch,
         name="series",
-    )(band, mine, far, twist, inverse_table)
-    operands = [resident(value) for value in (starts, series, outer, fraction, weights, sums)]
-    operands += [twist, inverse_table]
+    )(band, mine, far, twist, inverse_table, starts, shifts, fraction, weights, sums)
+    operands = [starts, resident(series), resident(outer), shifts, fraction, weights, twist, inverse_table]
+    operands += [resident(partial)]
     samples = pl.pallas_call(
         resample_kernel,
-        out_shape=pltpu.VMEM((owners, 2 * slot + ROWS, LANES), f32),
+        out_shape=payload,
         in_specs=[smem] + [vmem()] * len(operands),
         out_specs=vmem(),
         scratch_shapes=[
             pltpu.VMEM((2, LANES, LANES), f32),
             pltpu.VMEM((time_rows, LANES), f32),
             pltpu.VMEM((tmpl_local * owners * ROWS, LANES), f32),
-            pltpu.SMEM((tmpl_local * SFT_DEV, LANES), jnp.int32),
-            pltpu.SemaphoreType.DMA,
-        ],
+        ]
+        + scratch,
+        input_output_aliases={len(operands): 0},
         name="resample",
     )(band, *operands)
     samples = lax.all_to_all(samples, axes, split_axis=0, concat_axis=0, tiled=True)

time: 52.7 us -> 51.3 us (0.973)
  Pallas kernels: 6.84 us -> 6.04 us
  waiting for transfers between devices: 15.2 us -> 14.5 us
    pallas_call x2, Pallas kernels: 2.92 us -> 2.11 us  [the longest x1 1.22 us: run_device(): pl.pallas_call(series_kernel, out_shape=(pltpu.VMEM((time_rows, LANES), f...]
    ppermute x1, waiting for transfers between devices: 0.81 us -> 0.17 us  [run_device(): outer = lax.ppermute(edge, axes, along)]
  transfers between devices with their start and end apart: 3 -> 3, of which waited for: 3 -> 3; matrix products, arithmetic and copies ran while one was open for 1% -> 1% of each run, Pallas kernels for 4% -> 6%
where the time goes in v4:
time: 51.3 us; the launch traced here: 51 us
  blocking collectives  19.3 us (38%)
  waiting for transfers between devices  14.5 us (28%)
  starting transfers between devices  10.2 us (20%)
  Pallas kernels  6.04 us (12%)
  other arithmetic  0.69 us (1%)
    all_to_all x1, blocking collectives, run_device(): lax.all_to_all(samples, axes, split_axis=0, concat_axis=0, tiled=True)  19.3 us
    all_to_all x1, waiting for transfers between devices, run_device(): parts = lax.all_to_all(parts, axes, split_axis=0, concat_axis=0, tiled=True)  12.3 us
    ppermute x1, starting transfers between devices, run_device(): outer = lax.ppermute(edge, axes, along)  3.73 us
    all_to_all x1, starting transfers between devices, run_device(): parts = lax.all_to_all(parts, axes, split_axis=0, concat_axis=0, tiled=True)  3.49 us
    ppermute x1, starting transfers between devices, run_device(): far = lax.ppermute(sft_bins, 'band', [(0, 1), (1, 0)])  2.97 us
    ppermute x1, waiting for transfers between devices, run_device(): far = lax.ppermute(sft_bins, 'band', [(0, 1), (1, 0)])  2.05 us
    pallas_call x1, Pallas kernels, run_device(): pl.pallas_call(prepare_kernel, out_shape=(pltpu.VMEM((tmpl_local * SFT_DE...  1.63 us
    pallas_call x1, Pallas kernels, run_device(): pl.pallas_call(functools.partial(statistic_kernel, sample_total), out_sha...  1.3 us
  transfers between devices with their start and end apart: 3, of which 3 were waited for; matrix products, arithmetic and copies ran while one was open for 1% of the time, Pallas kernels for 6%

profile of v4, /device:TPU:0, one launch (start us, length us, event | category | flops | bytes accessed | tf_op | source)
XLA Modules:
  0.0 51.0 jit_solution(7052673127136516675)
XLA Ops:
  0.0 3.0 %collective-permute-start = (f32[2,16,1024]{2,1,0:T(8,128)}, f32[2,16,1024]{2,1,0:T(8,128)S(1)}, u32[]{:S(2)}, u32[]{:S(2)}) collective-permute-start(f32[2,16,1024]{2,1,0:T(8,128)} %bins_ref.1), channel_id=1, source_target_pairs={{0,2},{2,0},{1,3},{3,1},{4,6},{6,4},{5,7},{7,5},{8,10},{10,8},{9,1... | collective-permute-start | bytes 393224 | tf_op jit(solution)/shard_map/ppermute | solution.py:621
  3.0 1.6 %prepare.1 = (f32[256,128]{1,0:T(8,128)S(1)}, f32[512,128]{1,0:T(8,128)S(1)}, f32[8,128]{1,0:T(8,128)S(1)}, s32[16,128]{1,0:T(8,128)S(1)}, s32[128,128]{1,0:T(8,128)S(1)}, /*index=5*/f32[2,16,1024]{2,1,0:T(8,128)S(1)}) custom-call(s32[2,128,128]{2,1,0:T(8,128)} %code_ref.1, f32[2,2,128,128]{3,2,1,0:T(8,128)} %antenna_ref.1, f32[2,16,1024]{2,1,0:T(8,128)} %bins_ref.1), custom_call_target="tpu_custom_call" | custom-call | tf_op jit(solution)/shard_map/prepare/pallas_call | solution.py:622
  4.6 0.0 copy-start
  4.6 2.1 %collective-permute-done.far_ref = f32[2,16,1024]{2,1,0:T(8,128)S(1)} collective-permute-done((f32[2,16,1024]{2,1,0:T(8,128)}, f32[2,16,1024]{2,1,0:T(8,128)S(1)}, u32[]{:S(2)}, u32[]{:S(2)}) %collective-permute-start) | collective-permute-done | bytes 131104 | tf_op jit(solution)/shard_map/ppermute | solution.py:621
  6.7 0.0 copy-start.2
  6.7 3.7 %collective-permute-start.1 = (f32[2,16,128]{2,1,0:T(8,128)S(1)}, f32[2,16,128]{2,1,0:T(8,128)S(1)}, u32[]{:S(2)}, u32[]{:S(2)}) collective-permute-start(f32[2,16,128]{2,1,0:T(8,128)S(1)} %pack.1), channel_id=1, source_target_pairs={{0,4},{4,8},{8,12},{6,2},{10,6},{14,10},{1,5},{5,9},{9,13},{7,3},{... | collective-permute-start | bytes 49160 | tf_op jit(solution)/shard_map/ppermute | solution.py:646
  10.4 0.0 copy-done
  10.4 0.0 copy-done.2
  10.5 1.2 %series.1 = (f32[320,128]{1,0:T(8,128)S(1)}, f32[8,136,128]{2,1,0:T(8,128)S(1)}) custom-call(s32[1]{0:T(128)} %bitcast.band_ref, f32[2,16,1024]{2,1,0:T(8,128)S(1)} %get-tuple-element.16.mine_ref, f32[2,16,1024]{2,1,0:T(8,128)S(1)} %collective-permute-done.far_ref, f32[2,16,128]{2,1,0:T(8,128)S(1)} %copy-done.2, bf16[2,256,256]{2,1,0:T(8,128)(2,1)S(1)} %copy-done, ...), custom_call_target="tpu_custom_call" | custom-call | tf_op jit(solution)/shard_map/series/pallas_call | solution.py:656
  11.7 0.2 collective-permute-done.1.outer_ref
  11.9 0.9 %resample.1 = f32[8,136,128]{2,1,0:T(8,128)S(1)} custom-call(s32[1]{0:T(128)} %bitcast.band_ref, s32[16,128]{1,0:T(8,128)S(1)} %get-tuple-element.15.start_in_ref, f32[320,128]{1,0:T(8,128)S(1)} %get-tuple-element.21.series_ref, f32[2,16,128]{2,1,0:T(8,128)S(1)} %collective-permute-done.1.outer_ref, ...), custom_call_target="tpu_custom_call", output_to_operand_aliasing={{}: (9, {})} | custom-call | tf_op jit(solution)/shard_map/resample/pallas_call | solution.py:670
  12.8 19.3 %all_to_all.10.samples_ref = f32[8,136,128]{2,1,0:T(8,128)S(1)} all-to-all(f32[8,136,128]{2,1,0:T(8,128)S(1)} %resample.1), channel_id=1, replica_groups=mesh['groups'=2,'tm'=4,'band'=2,'tmpl'=2] {'tm','band'}, dimensions={0} | all-to-all | bytes 1114112 | tf_op jit(solution)/shard_map/all_to_all | solution.py:684
  32.1 1.0 %section.1 = (f32[8,128,128]{2,1,0:T(8,128)}, f32[8,128]{1,0:T(8,128)S(1)}) custom-call(f32[8,136,128]{2,1,0:T(8,128)S(1)} %all_to_all.10.samples_ref), custom_call_target="tpu_custom_call" | custom-call | tf_op jit(solution)/shard_map/section/pallas_call | solution.py:685
  33.1 3.5 %all-to-all-start.1 = ((f32[8,128,128]{2,1,0:T(8,128)}), f32[8,128,128]{2,1,0:T(8,128)S(1)}, u32[]{:S(2)}, u32[]{:S(2)}) async-start(f32[8,128,128]{2,1,0:T(8,128)} %get-tuple-element.23), calls=%async_computation.1 | async-start | bytes 1048576 | tf_op jit(solution)/shard_map/all_to_all | solution.py:693
  36.7 0.6 %fusion.9 = (f32[1,128,128]{2,1,0:T(8,128)S(1)}, f32[1,128,128]{2,1,0:T(8,128)S(1)}, f32[1,128,128]{2,1,0:T(8,128)S(1)}, f32[1,128,128]{2,1,0:T(8,128)S(1)}) fusion(s32[128]{0:T(128)S(1)} %iota_shift-right-logical_fusion, s32[128]{0:T(128)S(1)} %broadcast_add_fusion.1, pred[128]{0:T(512)(128)(4,1)S(1)} %compare_and_fusion.1, s32[128]{0:T(128)S(1)} %iota_and_fusion, ...), kind=kLoop, calls=%fused_computation.20 | loop fusion | flops 557056 | bytes 264452 | tf_op jit(solution)/shard_map/cos | solution.py:42
  37.3 0.0 copy-start.1
  37.4 12.3 %all-to-all-done.1.parts_ref = f32[8,128,128]{2,1,0:T(8,128)S(1)} async-done(((f32[8,128,128]{2,1,0:T(8,128)}), f32[8,128,128]{2,1,0:T(8,128)S(1)}, u32[]{:S(2)}, u32[]{:S(2)}) %all-to-all-start.1) | async-done | bytes 524320 | tf_op jit(solution)/shard_map/all_to_all | solution.py:693
  49.7 0.0 copy-done.1
  49.7 1.3 %statistic.1 = f32[2,128,128]{2,1,0:T(8,128)} custom-call(f32[8,128,128]{2,1,0:T(8,128)S(1)} %all-to-all-done.1.parts_ref, f32[8,128]{1,0:T(8,128)S(1)} %get-tuple-element.24.sums_ref, f32[2,128,128]{2,1,0:T(8,128)S(1)} %get-tuple-element.29.coarse_ref, f32[2,128,128]{2,1,0:T(8,128)S(1)} %get-tuple-element.30.fine_ref, bf16[2,256,256]{2,1,0:T(8,128)(2,1)S(1)} %copy-done.1), custom_call_target="tpu_custom_call" | custom-call | tf_op jit(solution)/shard_map/statistic/pallas_call | solution.py:701
  (8 shorter events, 0.1 us)
Async XLA Ops:
  0.0 6.7 %collective-permute-start = (f32[2,16,1024]{2,1,0:T(8,128)}, f32[2,16,1024]{2,1,0:T(8,128)S(1)}, u32[]{:S(2)}, u32[]{:S(2)}) collective-permute-start(f32[2,16,1024]{2,1,0:T(8,128)} %bins_ref.1), channel_id=1, source_target_pairs={{0,2},{2,0},{1,3},{3,1},{4,6},{6,4},{5,7},{7,5},{8,10},{10,8},{9,1... | collective-permute-start | bytes 393224 | tf_op jit(solution)/shard_map/ppermute | solution.py:621
  4.6 5.8 %copy-start = (bf16[2,256,256]{2,1,0:T(8,128)(2,1)S(1)}, bf16[2,256,256]{2,1,0:T(8,128)(2,1)}, u32[]{:S(2)}) copy-start(bf16[2,256,256]{2,1,0:T(8,128)(2,1)} %constant.84.clone.table_ref) | copy-start | bytes 786436
  6.7 3.8 %copy-start.2 = (f32[2,16,128]{2,1,0:T(8,128)S(1)}, f32[2,16,128]{2,1,0:T(8,128)}, u32[]{:S(2)}) copy-start(f32[2,16,128]{2,1,0:T(8,128)} %constant.83.clone.twist_ref) | copy-start | bytes 49156
  6.7 5.2 %collective-permute-start.1 = (f32[2,16,128]{2,1,0:T(8,128)S(1)}, f32[2,16,128]{2,1,0:T(8,128)S(1)}, u32[]{:S(2)}, u32[]{:S(2)}) collective-permute-start(f32[2,16,128]{2,1,0:T(8,128)S(1)} %pack.1), channel_id=1, source_target_pairs={{0,4},{4,8},{8,12},{6,2},{10,6},{14,10},{1,5},{5,9},{9,13},{7,3},{... | collective-permute-start | bytes 49160 | tf_op jit(solution)/shard_map/ppermute | solution.py:646
  33.1 16.6 %all-to-all-start.1 = ((f32[8,128,128]{2,1,0:T(8,128)}), f32[8,128,128]{2,1,0:T(8,128)S(1)}, u32[]{:S(2)}, u32[]{:S(2)}) async-start(f32[8,128,128]{2,1,0:T(8,128)} %get-tuple-element.23), calls=%async_computation.1 | async-start | bytes 1048576 | tf_op jit(solution)/shard_map/all_to_all | solution.py:693
  37.3 12.4 %copy-start.1 = (bf16[2,256,256]{2,1,0:T(8,128)(2,1)S(1)}, bf16[2,256,256]{2,1,0:T(8,128)(2,1)}, u32[]{:S(2)}) copy-start(bf16[2,256,256]{2,1,0:T(8,128)(2,1)} %constant.85.clone.table_ref) | copy-start | bytes 786436

commit v5 on v4

--- a/solution.py
+++ b/solution.py
@@ -633,7 +633,17 @@
         out_specs=(vmem(),) * 6,
         name="prepare",
     )(delay_code, antenna, sft_bins)
+    row = lax.broadcasted_iota(jnp.int32, (2 * owners * ROWS, LANES), 0)
+    lane = lax.broadcasted_iota(jnp.int32, (2 * owners * ROWS, LANES), 1)
+    freq = my_rank + owners * (row % ROWS)
+    coarse = jnp.stack(phase_pair((row // ROWS) * freq, sample_total // LANES, -1.0))
+    fine = jnp.stack(phase_pair(lane * (freq + owners * SFT_DEV * (row // ROWS)), sample_total, -1.0))
+    fine = fine * (1.0 / math.sqrt(sample_total))
+    last_table = jnp.asarray(forward_table())
+    coarse, fine, last_table = resident(coarse), resident(fine), resident(last_table)
     far, mine = resident(far), resident(mine)
+    mine, coarse, fine, last_table = lax.optimization_barrier((mine, coarse, fine, last_table))
+    mine = resident(mine)
     edge = pl.pallas_call(
         pack_kernel,
         out_shape=pltpu.VMEM((2, NP, LANES), f32),
@@ -690,14 +700,8 @@
         scratch_shapes=[pltpu.VMEM((2, owners * slot, LANES), f32)],
         name="section",
     )(resident(samples))
-    parts = lax.all_to_all(parts, axes, split_axis=0, concat_axis=0, tiled=True)
-    row = lax.broadcasted_iota(jnp.int32, (2 * owners * ROWS, LANES), 0)
-    lane = lax.broadcasted_iota(jnp.int32, (2 * owners * ROWS, LANES), 1)
-    freq = my_rank + owners * (row % ROWS)
-    coarse = jnp.stack(phase_pair((row // ROWS) * freq, sample_total // LANES, -1.0))
-    fine = jnp.stack(phase_pair(lane * (freq + owners * SFT_DEV * (row // ROWS)), sample_total, -1.0))
-    fine = fine * (1.0 / math.sqrt(sample_total))
-    operands = [parts, totals, coarse, fine, jnp.asarray(forward_table())]
+    parts = lax.all_to_all(resident(parts), axes, split_axis=0, concat_axis=0, tiled=True)
+    operands = [parts, totals, coarse, fine, last_table]
     f_stat = pl.pallas_call(
         functools.partial(statistic_kernel, sample_total),
         out_shape=jax.ShapeDtypeStruct((tmpl_local, NQ, LANES), f32),

time: 51.3 us -> 50.4 us (0.982)
  blocking collectives: 19.3 us -> 35.8 us
  waiting for transfers between devices: 14.5 us -> 1.49 us
  starting transfers between devices: 10.2 us -> 6.7 us
  Pallas kernels: 6.04 us -> 5.33 us
    all_to_all x0 -> x1, blocking collectives: none -> 16.5 us  [run_device(): lax.all_to_all(resident(parts), axes, split_axis=0, concat_axis=0, tiled=...]
    all_to_all x1 -> x0, waiting for transfers between devices: 12.3 us -> none  [run_device(): parts = lax.all_to_all(parts, axes, split_axis=0, concat_axis=0, tiled=True)]
    all_to_all x1 -> x0, starting transfers between devices: 3.49 us -> none  [run_device(): parts = lax.all_to_all(parts, axes, split_axis=0, concat_axis=0, tiled=True)]
    ppermute x1, waiting for transfers between devices: 2.05 us -> 1.32 us  [run_device(): far = lax.ppermute(sft_bins, 'band', [(0, 1), (1, 0)])]
    pallas_call x1, Pallas kernels: 0.99 us -> 0.27 us  [run_device(): pl.pallas_call(section_kernel, out_shape=(pltpu.VMEM((owners, 2 * slot, L...]
  transfers between devices with their start and end apart: 3 -> 2, of which waited for: 3 -> 2; matrix products, arithmetic and copies ran while one was open for 1% -> 1% of each run, Pallas kernels for 6% -> 6%
where the time goes in v5:
time: 50.4 us; the launch traced here: 50.2 us
  blocking collectives  35.8 us (71%)
  starting transfers between devices  6.7 us (13%)
  Pallas kernels  5.33 us (11%)
  waiting for transfers between devices  1.49 us (3%)
  other arithmetic  0.69 us (1%)
    all_to_all x1, blocking collectives, run_device(): lax.all_to_all(samples, axes, split_axis=0, concat_axis=0, tiled=True)  19.3 us
    all_to_all x1, blocking collectives, run_device(): lax.all_to_all(resident(parts), axes, split_axis=0, concat_axis=0, tiled=...  16.5 us
    ppermute x1, starting transfers between devices, run_device(): outer = lax.ppermute(edge, axes, along)  3.73 us
    ppermute x1, starting transfers between devices, run_device(): far = lax.ppermute(sft_bins, 'band', [(0, 1), (1, 0)])  2.97 us
    pallas_call x1, Pallas kernels, run_device(): pl.pallas_call(prepare_kernel, out_shape=(pltpu.VMEM((tmpl_local * SFT_DE...  1.63 us
    ppermute x1, waiting for transfers between devices, run_device(): far = lax.ppermute(sft_bins, 'band', [(0, 1), (1, 0)])  1.32 us
    pallas_call x1, Pallas kernels, run_device(): pl.pallas_call(functools.partial(statistic_kernel, sample_total), out_sha...  1.29 us
    pallas_call x1, Pallas kernels, run_device(): pl.pallas_call(series_kernel, out_shape=(pltpu.VMEM((time_rows, LANES), f...  1.22 us
  transfers between devices with their start and end apart: 2, of which 2 were waited for; matrix products, arithmetic and copies ran while one was open for 1% of the time, Pallas kernels for 6%

profile of v5, /device:TPU:0, one launch (start us, length us, event | category | flops | bytes accessed | tf_op | source)
XLA Modules:
  0.0 50.2 jit_solution(17891268795041103927)
XLA Ops:
  0.0 3.0 %collective-permute-start = (f32[2,16,1024]{2,1,0:T(8,128)}, f32[2,16,1024]{2,1,0:T(8,128)S(1)}, u32[]{:S(2)}, u32[]{:S(2)}) collective-permute-start(f32[2,16,1024]{2,1,0:T(8,128)} %bins_ref.1), channel_id=1, source_target_pairs={{0,2},{2,0},{1,3},{3,1},{4,6},{6,4},{5,7},{7,5},{8,10},{10,8},{9,1... | collective-permute-start | bytes 393224 | tf_op jit(solution)/shard_map/ppermute | solution.py:621
  3.0 0.6 %fusion.9 = (f32[1,128,128]{2,1,0:T(8,128)S(1)}, f32[1,128,128]{2,1,0:T(8,128)S(1)}, f32[1,128,128]{2,1,0:T(8,128)S(1)}, f32[1,128,128]{2,1,0:T(8,128)S(1)}) fusion(s32[128]{0:T(128)S(1)} %iota_shift-right-logical_fusion, s32[128]{0:T(128)S(1)} %broadcast_add_fusion.1, pred[128]{0:T(512)(128)(4,1)S(1)} %compare_and_fusion.1, s32[128]{0:T(128)S(1)} %iota_and_fusion, ...), kind=kLoop, calls=%fused_computation.20 | loop fusion | flops 557056 | bytes 264452 | tf_op jit(solution)/shard_map/cos | solution.py:42
  3.7 1.6 %prepare.1 = (f32[256,128]{1,0:T(8,128)S(1)}, f32[512,128]{1,0:T(8,128)S(1)}, f32[8,128]{1,0:T(8,128)S(1)}, s32[16,128]{1,0:T(8,128)S(1)}, s32[128,128]{1,0:T(8,128)S(1)}, /*index=5*/f32[2,16,1024]{2,1,0:T(8,128)S(1)}) custom-call(s32[2,128,128]{2,1,0:T(8,128)} %code_ref.1, f32[2,2,128,128]{3,2,1,0:T(8,128)} %antenna_ref.1, f32[2,16,1024]{2,1,0:T(8,128)} %bins_ref.1), custom_call_target="tpu_custom_call" | custom-call | tf_op jit(solution)/shard_map/prepare/pallas_call | solution.py:622
  5.3 0.0 copy-start
  5.4 1.3 %collective-permute-done.far_ref = f32[2,16,1024]{2,1,0:T(8,128)S(1)} collective-permute-done((f32[2,16,1024]{2,1,0:T(8,128)}, f32[2,16,1024]{2,1,0:T(8,128)S(1)}, u32[]{:S(2)}, u32[]{:S(2)}) %collective-permute-start) | collective-permute-done | bytes 131104 | tf_op jit(solution)/shard_map/ppermute | solution.py:621
  6.7 0.0 copy-start.2
  6.7 3.7 %collective-permute-start.1 = (f32[2,16,128]{2,1,0:T(8,128)S(1)}, f32[2,16,128]{2,1,0:T(8,128)S(1)}, u32[]{:S(2)}, u32[]{:S(2)}) collective-permute-start(f32[2,16,128]{2,1,0:T(8,128)S(1)} %pack.1), channel_id=1, source_target_pairs={{0,4},{4,8},{8,12},{6,2},{10,6},{14,10},{1,5},{5,9},{9,13},{7,3},{... | collective-permute-start | bytes 49160 | tf_op jit(solution)/shard_map/ppermute | solution.py:656
  10.4 0.0 copy-done
  10.4 0.0 copy-done.2
  10.5 1.2 %series.1 = (f32[320,128]{1,0:T(8,128)S(1)}, f32[8,136,128]{2,1,0:T(8,128)S(1)}) custom-call(s32[1]{0:T(128)} %bitcast.band_ref, f32[2,16,1024]{2,1,0:T(8,128)S(1)} %get-tuple-element.21.mine_ref, f32[2,16,1024]{2,1,0:T(8,128)S(1)} %collective-permute-done.far_ref, f32[2,16,128]{2,1,0:T(8,128)S(1)} %copy-done.2, bf16[2,256,256]{2,1,0:T(8,128)(2,1)S(1)} %copy-done, ...), custom_call_target="tpu_custom_call" | custom-call | tf_op jit(solution)/shard_map/series/pallas_call | solution.py:666
  11.7 0.2 collective-permute-done.1.outer_ref
  11.9 0.9 %resample.1 = f32[8,136,128]{2,1,0:T(8,128)S(1)} custom-call(s32[1]{0:T(128)} %bitcast.band_ref, s32[16,128]{1,0:T(8,128)S(1)} %get-tuple-element.19.start_in_ref, f32[320,128]{1,0:T(8,128)S(1)} %get-tuple-element.26.series_ref, f32[2,16,128]{2,1,0:T(8,128)S(1)} %collective-permute-done.1.outer_ref, ...), custom_call_target="tpu_custom_call", output_to_operand_aliasing={{}: (9, {})} | custom-call | tf_op jit(solution)/shard_map/resample/pallas_call | solution.py:680
  12.8 19.3 %all_to_all.10.samples_ref = f32[8,136,128]{2,1,0:T(8,128)S(1)} all-to-all(f32[8,136,128]{2,1,0:T(8,128)S(1)} %resample.1), channel_id=1, replica_groups=mesh['groups'=2,'tm'=4,'band'=2,'tmpl'=2] {'tm','band'}, dimensions={0} | all-to-all | bytes 1114112 | tf_op jit(solution)/shard_map/all_to_all | solution.py:694
  32.1 0.3 section.1
  32.4 0.0 copy-start.1
  32.4 16.5 %all_to_all.11.parts_ref = f32[8,128,128]{2,1,0:T(8,128)S(1)} all-to-all(f32[8,128,128]{2,1,0:T(8,128)S(1)} %get-tuple-element.28), channel_id=1, replica_groups=mesh['groups'=2,'tm'=4,'band'=2,'tmpl'=2] {'tm','band'}, dimensions={0} | all-to-all | bytes 1048576 | tf_op jit(solution)/shard_map/all_to_all | solution.py:703
  48.9 0.0 copy-done.1
  48.9 1.3 %statistic.1 = f32[2,128,128]{2,1,0:T(8,128)} custom-call(f32[8,128,128]{2,1,0:T(8,128)S(1)} %all_to_all.11.parts_ref, f32[8,128]{1,0:T(8,128)S(1)} %get-tuple-element.29.sums_ref, f32[2,128,128]{2,1,0:T(8,128)S(1)} %get-tuple-element.30.coarse_ref, f32[2,128,128]{2,1,0:T(8,128)S(1)} %get-tuple-element.31.fine_ref, bf16[2,256,256]{2,1,0:T(8,128)(2,1)S(1)} %copy-done.1), custom_call_target="tpu_custom_call" | custom-call | tf_op jit(solution)/shard_map/statistic/pallas_call | solution.py:705
  (8 shorter events, 0.1 us)
Async XLA Ops:
  0.0 6.7 %collective-permute-start = (f32[2,16,1024]{2,1,0:T(8,128)}, f32[2,16,1024]{2,1,0:T(8,128)S(1)}, u32[]{:S(2)}, u32[]{:S(2)}) collective-permute-start(f32[2,16,1024]{2,1,0:T(8,128)} %bins_ref.1), channel_id=1, source_target_pairs={{0,2},{2,0},{1,3},{3,1},{4,6},{6,4},{5,7},{7,5},{8,10},{10,8},{9,1... | collective-permute-start | bytes 393224 | tf_op jit(solution)/shard_map/ppermute | solution.py:621
  5.3 5.1 %copy-start = (bf16[2,256,256]{2,1,0:T(8,128)(2,1)S(1)}, bf16[2,256,256]{2,1,0:T(8,128)(2,1)}, u32[]{:S(2)}) copy-start(bf16[2,256,256]{2,1,0:T(8,128)(2,1)} %constant.85.clone.table_ref) | copy-start | bytes 786436
  6.7 3.8 %copy-start.2 = (f32[2,16,128]{2,1,0:T(8,128)S(1)}, f32[2,16,128]{2,1,0:T(8,128)}, u32[]{:S(2)}) copy-start(f32[2,16,128]{2,1,0:T(8,128)} %constant.84.clone.twist_ref) | copy-start | bytes 49156
  6.7 5.2 %collective-permute-start.1 = (f32[2,16,128]{2,1,0:T(8,128)S(1)}, f32[2,16,128]{2,1,0:T(8,128)S(1)}, u32[]{:S(2)}, u32[]{:S(2)}) collective-permute-start(f32[2,16,128]{2,1,0:T(8,128)S(1)} %pack.1), channel_id=1, source_target_pairs={{0,4},{4,8},{8,12},{6,2},{10,6},{14,10},{1,5},{5,9},{9,13},{7,3},{... | collective-permute-start | bytes 49160 | tf_op jit(solution)/shard_map/ppermute | solution.py:656
  32.4 16.5 %copy-start.1 = (bf16[2,256,256]{2,1,0:T(8,128)(2,1)S(1)}, bf16[2,256,256]{2,1,0:T(8,128)(2,1)}, u32[]{:S(2)}) copy-start(bf16[2,256,256]{2,1,0:T(8,128)(2,1)} %constant.83.clone.table_ref) | copy-start | bytes 786436
